TPU v7x, 32 devices: a whole 2x2x4 slice. The times are simulated.
32 devices in a mesh: parts: 2 (over y), mp: 4 (over z), split: 4 (over x, core).
Axes of the slice: x: 2, y: 2, z: 4, core: 2. Of those that a mesh axis runs over, the one named last changes fastest.
Arguments:
- tokens: bfloat16 [384, 5120], P(('parts', 'mp'), 'split'), parts along dimension 0, may hold values from -6 to 6
- lengths: int32 [6], P('parts'), parts along dimension 0, may hold values from 1 to 64
- teacher_gate: bfloat16 [10240, 13824], P(('parts', 'split'), 'mp'), parts along dimension 0, may hold values from -0.078125 to 0.078125
- teacher_up: bfloat16 [10240, 13824], P(('parts', 'split'), 'mp'), parts along dimension 0, may hold values from -0.078125 to 0.078125
- teacher_down: bfloat16 [27648, 5120], P(('parts', 'mp'), 'split'), parts along dimension 0, may hold values from -0.0546875 to 0.0546875
- first_gate: bfloat16 [10240, 6912], P(('parts', 'split'), 'mp'), parts along dimension 0, may hold values from -0.078125 to 0.078125
- first_up: bfloat16 [10240, 6912], P(('parts', 'split'), 'mp'), parts along dimension 0, may hold values from -0.078125 to 0.078125
- first_down: bfloat16 [13824, 5120], P(('parts', 'mp'), 'split'), parts along dimension 0, may hold values from -0.078125 to 0.078125
- second_gate: bfloat16 [10240, 5632], P(('parts', 'split'), 'mp'), parts along dimension 0, may hold values from -0.078125 to 0.078125
- second_up: bfloat16 [10240, 5632], P(('parts', 'split'), 'mp'), parts along dimension 0, may hold values from -0.078125 to 0.078125
- second_down: bfloat16 [11264, 5120], P(('parts', 'mp'), 'split'), parts along dimension 0, may hold values from -0.078125 to 0.078125
Outputs:
- grad_first_gate: bfloat16 [10240, 6912], P(('parts', 'split'), 'mp'), parts along dimension 0
- grad_first_up: bfloat16 [10240, 6912], P(('parts', 'split'), 'mp'), parts along dimension 0
- grad_first_down: bfloat16 [13824, 5120], P(('parts', 'mp'), 'split'), parts along dimension 0
- grad_second_gate: bfloat16 [10240, 5632], P(('parts', 'split'), 'mp'), parts along dimension 0
- grad_second_up: bfloat16 [10240, 5632], P(('parts', 'split'), 'mp'), parts along dimension 0
- grad_second_down: bfloat16 [11264, 5120], P(('parts', 'mp'), 'split'), parts along dimension 0
- losses: float32 [4], P('parts'), parts along dimension 0
There are 2 independent parts, one for each index of `parts`. A program takes and returns all parts, laid end to end along the dimension named above; each array names one. Nothing has to cross between parts.
All inputs are finite; a program needn't handle non-finite values.
Results may differ from a plain program's by a relative error of at most 0.0065.
Values may be sent and summed in bfloat16 or wider, within the bound.
A program may use at most 128 MiB of HBM per device.

v0:
```python
import functools

import jax
import jax.numpy as jnp
from jax import lax
from jax.experimental import pallas as pl
from jax.experimental.pallas import tpu as pltpu
from jax.sharding import PartitionSpec as P

MESH = pl.DeviceIdType.MESH
VMEM = pl.BlockSpec(memory_space=pltpu.VMEM)
ANY = pl.BlockSpec(memory_space=pl.ANY)
TILE = 384
GRANT = 60 * 2**20

LEN = 64


def contract_rows(left, right):
    return lax.dot_general(
        left, right, (((0,), (0,)), ((), ())), preferred_element_type=jnp.float32
    )


def valid_rows(lengths, count):
    position = jnp.arange(count, dtype=jnp.int32)
    seq_ids = position // LEN
    within = position - seq_ids * LEN
    limit = jnp.sum(
        jnp.where(
            seq_ids[:, None] == jnp.arange(lengths.shape[0], dtype=jnp.int32)[None, :],
            lengths[None, :],
            0,
        ),
        axis=1,
    )
    return (within < limit).astype(jnp.float32)[:, None]


def activate(gate, up):
    return (jax.nn.silu(gate) * up).astype(jnp.bfloat16)


def hidden_grads(back, gate, up):
    sig = jax.nn.sigmoid(gate)
    dgate = (back * up * sig * (1.0 + gate * (1.0 - sig))).astype(jnp.bfloat16)
    dup = (back * gate * sig).astype(jnp.bfloat16)
    return (dgate, dup)


class Links:
    def __init__(self, send, recv):
        self.send, self.recv, self.made = send, recv, []

    def copy(self, src, dst, device):
        at = len(self.made)
        made = pltpu.make_async_remote_copy(
            src_ref=src,
            dst_ref=dst,
            send_sem=self.send.at[at],
            recv_sem=self.recv.at[at],
            device_id=device,
            device_id_type=MESH,
        )
        made.start()
        self.made.append(made)
        return made

    def drain(self):
        for made in self.made:
            made.wait_send()


def greet(devices):
    barrier = pltpu.get_barrier_semaphore()
    for device in devices:
        pl.semaphore_signal(barrier, inc=1, device_id=device, device_id_type=MESH)
    pl.semaphore_wait(barrier, len(devices))


def tiles(width, body):
    full = width // TILE
    if full:

        @pl.loop(0, full)
        def _(i):
            body(pl.ds(pl.multiple_of(i * TILE, 128), TILE))

    if width % TILE:
        body(pl.ds(full * TILE, width % TILE))


def four_places(axis):
    me = lax.axis_index(axis)
    chip, core = me // 2, me % 2
    sib = chip * 2 + (1 - core)
    far = (1 - chip) * 2 + core
    diag = (1 - chip) * 2 + (1 - core)
    return me, sib, far, diag


def rows_at(block, count):
    return pl.ds(pl.multiple_of(block * count, 16), count)


class Unit:
    def __init__(self, links, sib, far, refs):
        self.links, self.sib, self.far = links, sib, far
        self.snd1, self.own, self.rcv1, self.snd2, self.rcv2 = refs
        self.half = self.snd1.shape[0] // 2
        self.width = self.snd1.shape[1]

    def multiply(self, left, weight, transposed):
        def body(cols):
            if transposed:
                right, dims = weight[cols, :], (((1,), (1,)), ((), ()))
            else:
                right, dims = weight[:, cols], (((1,), (0,)), ((), ()))
            out = lax.dot_general(left[...], right, dims, preferred_element_type=jnp.float32)
            pair = 2 * self.half
            self.snd1[:, cols] = out[:pair].astype(jnp.bfloat16)
            self.own[:, cols] = out[pair:]

        tiles(self.width, body)
        self.first = self.links.copy(self.snd1, self.rcv1, {"split": self.sib})

    def forward(self):
        self.first.wait_recv()
        half = self.half

        def body(cols):
            both = self.own[:half, cols] + self.rcv1[:half, cols].astype(jnp.float32)
            self.snd2[:, cols] = both.astype(jnp.bfloat16)

        tiles(self.width, body)
        self.second = self.links.copy(self.snd2, self.rcv2, {"split": self.far})

    def ready(self):
        self.second.wait_recv()

    def value(self, cols):
        half = self.half
        return (
            self.own[half:, cols]
            + self.rcv1[half:, cols].astype(jnp.float32)
            + self.rcv2[:, cols].astype(jnp.float32)
        )


def unit_scratch(rows, width):
    half, pair = rows // 4, rows // 2
    return [
        pltpu.VMEM((pair, width), jnp.bfloat16),
        pltpu.VMEM((pair, width), jnp.float32),
        pltpu.VMEM((pair, width), jnp.bfloat16),
        pltpu.VMEM((half, width), jnp.bfloat16),
        pltpu.VMEM((half, width), jnp.bfloat16),
    ]


class Spread:
    def __init__(self, links, ref, count, places, axis="split", source=None):
        me, self.sib, self.far = places[:3]
        self.links, self.ref, self.count, self.axis = links, ref, count, axis
        mine = ref.at[rows_at(me, count)]
        source = mine if source is None else source
        self.out = links.copy(source, mine, {axis: self.far})
        self.side = links.copy(source, mine, {axis: self.sib})

    def relay(self):
        self.out.wait_recv()
        theirs = self.ref.at[rows_at(self.far, self.count)]
        self.last = self.links.copy(theirs, theirs, {self.axis: self.sib})

    def finish(self):
        self.side.wait_recv()
        self.last.wait_recv()


def arrange(dst, src, order, count):
    for i, block in enumerate(order):
        dst[i * count : (i + 1) * count, :] = src[rows_at(block, count), :]


def forward_kernel(flips, *refs):
    tok, weights = refs[0], refs[1:7]
    gathered, hidden, kept = refs[7], refs[8:11], refs[11:15]
    xp, wbuf = refs[15], refs[16:22]
    send, recv, wsem = refs[-3:]
    scratch = refs[22:-3]
    loads = [pltpu.make_async_copy(weights[i], wbuf[i], wsem.at[i]) for i in range(6)]
    for load in loads:
        load.start()
    places, ring = four_places("split"), four_places("mp")
    me, sib, far, diag = places
    greet([{"split": p} for p in (sib, far)] + [{"mp": p} for p in ring[1:3]])
    links = Links(send, recv)
    block = tok.shape[0]
    count = gathered.shape[0] // 4
    moves = Spread(links, gathered, block, ring, "mp", tok)
    gathered[rows_at(ring[0], block), :] = tok[...]
    moves.relay()
    moves.finish()
    arrange(xp, gathered, (diag, sib, far, me), count)
    units = [Unit(links, sib, far, scratch[5 * i : 5 * i + 5]) for i in range(6)]

    def multiply(i):
        loads[i].wait()
        units[i].multiply(xp, wbuf[i], flips[i])

    spreads = [None] * 3

    def activate_rows(layer):
        gate, up = units[2 * layer], units[2 * layer + 1]
        gate.ready()
        up.ready()
        out = hidden[layer]

        def body(cols):
            g, u = gate.value(cols), up.value(cols)
            out[rows_at(me, count), cols] = (g * jax.nn.sigmoid(g) * u).astype(jnp.bfloat16)
            if layer < 2:
                kept[2 * layer][:, cols] = g
                kept[2 * layer + 1][:, cols] = u

        tiles(gate.width, body)
        spreads[layer] = Spread(links, out, count, places)

    multiply(0)
    multiply(1)
    units[0].forward()
    multiply(2)
    units[1].forward()
    multiply(3)
    units[2].forward()
    units[3].forward()
    multiply(4)
    units[4].forward()
    activate_rows(0)
    multiply(5)
    units[5].forward()
    activate_rows(1)
    spreads[0].relay()
    spreads[1].relay()
    activate_rows(2)
    spreads[2].relay()
    for spread in spreads:
        spread.finish()
    links.drain()


def forward_call(mp, tokens, weights, flips):
    block, depth = tokens.shape
    rows = block * mp
    count = rows // 4
    widths = [w.shape[0] if flip else w.shape[1] for w, flip in zip(weights, flips)]
    shape = jax.ShapeDtypeStruct
    outs = [shape((rows, depth), jnp.bfloat16)]
    outs += [shape((rows, widths[2 * i]), jnp.bfloat16) for i in range(3)]
    outs += [shape((count, widths[i]), jnp.float32) for i in range(4)]
    scratch = [pltpu.VMEM((rows, depth), jnp.bfloat16)]
    scratch += [pltpu.VMEM(w.shape, jnp.bfloat16) for w in weights]
    for width in widths:
        scratch += unit_scratch(rows, width)
    copies = 3 + 2 * 6 + 3 * 3
    scratch += [pltpu.SemaphoreType.DMA((copies,))] * 2 + [pltpu.SemaphoreType.DMA((6,))]
    return pl.pallas_call(
        functools.partial(forward_kernel, flips),
        out_shape=outs,
        in_specs=[VMEM] + [ANY] * 6,
        out_specs=[VMEM] * 8,
        scratch_shapes=scratch,
        compiler_params=pltpu.CompilerParams(
            collective_id=0, has_side_effects=True, vmem_limit_bytes=GRANT
        ),
    )(tokens, *weights)


def backward_kernel(*refs):
    diffs, scale, downs, kept = refs[0:2], refs[2], refs[3:5], refs[5:9]
    cots, grads, loss = refs[9:11], refs[11:15], refs[15]
    snds, rcvs, xps, wbuf = refs[16:18], refs[18:20], refs[20:22], refs[22:24]
    part, marked = refs[24:26]
    send, recv, wsem = refs[-3:]
    scratch = refs[26:-3]
    loads = [pltpu.make_async_copy(downs[i], wbuf[i], wsem.at[i]) for i in range(2)]
    for load in loads:
        load.start()
    places, ring = four_places("split"), four_places("mp")
    me, sib, far, diag = places
    greet([{"mp": p} for p in ring[1:]] + [{"split": p} for p in places[1:]])
    links = Links(send, recv)
    block = count = scale.shape[0] // 4
    mine = rows_at(ring[0], block)
    moves = []
    for diff, snd, rcv in zip(diffs, snds, rcvs):
        snd[...] = diff[...].astype(jnp.bfloat16)
        moves.append(
            [
                links.copy(snd.at[rows_at(p, block)], rcv.at[k], {"mp": p})
                for k, p in enumerate(ring[1:])
            ]
        )
    factor = scale[mine, 0:1]
    units = [Unit(links, sib, far, scratch[5 * i : 5 * i + 5]) for i in range(2)]
    turns, sums = [], []
    for diff, rcv, cot, made in zip(diffs, rcvs, cots, moves):
        total = diff[mine, :]
        for k, move in enumerate(made):
            move.wait_recv()
            total = total + rcv[k].astype(jnp.float32)
        scaled = factor * total
        cot[mine, :] = scaled.astype(jnp.bfloat16)
        turns.append(Spread(links, cot, block, ring, "mp"))
        sums.append(0.5 * jnp.sum(scaled * total, keepdims=True))
    row = lax.broadcasted_iota(jnp.int32, part.shape[1:], 0)
    part[0] = jnp.where(row == 0, sums[0], sums[1])
    parts = [links.copy(part.at[0], part.at[k], {"mp": ring[k]}) for k in (1, 2, 3)]

    def multiply(i):
        turns[i].finish()
        arrange(xps[i], cots[i], (diag, sib, far, me), count)
        loads[i].wait()
        units[i].multiply(xps[i], wbuf[i], True)

    spreads = []

    def differentiate(i):
        units[i].ready()

        def body(cols):
            back = units[i].value(cols)
            gate, up = kept[2 * i][:, cols], kept[2 * i + 1][:, cols]
            sig = jax.nn.sigmoid(gate)
            dgate = back * up * sig * (1.0 + gate * (1.0 - sig))
            grads[2 * i][rows_at(me, count), cols] = dgate.astype(jnp.bfloat16)
            grads[2 * i + 1][rows_at(me, count), cols] = (back * gate * sig).astype(jnp.bfloat16)

        tiles(units[i].width, body)
        spreads.extend(Spread(links, grads[2 * i + j], count, places) for j in range(2))

    turns[0].relay()
    turns[1].relay()
    multiply(0)
    for move in parts:
        move.wait_recv()
    marked[0] = part[0] + part[1] + part[2] + part[3]
    marks = [links.copy(marked.at[0], marked.at[k], {"split": places[k]}) for k in (1, 2, 3)]
    units[0].forward()
    multiply(1)
    units[1].forward()
    differentiate(0)
    differentiate(1)
    for mark in marks:
        mark.wait_recv()
    loss[...] = marked[0] + marked[1] + marked[2] + marked[3]
    for spread in spreads:
        spread.relay()
    for spread in spreads:
        spread.finish()
    links.drain()


def backward_call(diffs, scale, downs, kept):
    rows, width = diffs[0].shape
    block = rows // 4
    widths = [down.shape[0] for down in downs]
    shape = jax.ShapeDtypeStruct
    outs = [shape((rows, width), jnp.bfloat16)] * 2
    outs += [shape((rows, widths[i // 2]), jnp.bfloat16) for i in range(4)]
    outs.append(shape((8, 128), jnp.float32))
    scratch = [pltpu.VMEM((rows, width), jnp.bfloat16)] * 2
    scratch += [pltpu.VMEM((3, block, width), jnp.bfloat16)] * 2
    scratch += [pltpu.VMEM((rows, width), jnp.bfloat16)] * 2
    scratch += [pltpu.VMEM(down.shape, jnp.bfloat16) for down in downs]
    scratch += [pltpu.VMEM((4, 8, 128), jnp.float32)] * 2
    for w in widths:
        scratch += unit_scratch(rows, w)
    copies = 2 * 3 + 2 * 3 + 3 + 2 * 2 + 3 * 4 + 3
    scratch += [pltpu.SemaphoreType.DMA((copies,))] * 2 + [pltpu.SemaphoreType.DMA((2,))]
    return pl.pallas_call(
        backward_kernel,
        out_shape=outs,
        in_specs=[VMEM] * 3 + [ANY] * 2 + [VMEM] * 4,
        out_specs=[VMEM] * 7,
        scratch_shapes=scratch,
        compiler_params=pltpu.CompilerParams(
            collective_id=1, has_side_effects=True, vmem_limit_bytes=GRANT
        ),
    )(*diffs, scale, *downs, *kept)


def per_device_kernels(
    mp,
    tokens,
    lengths,
    teacher_gate,
    teacher_up,
    teacher_down,
    first_gate,
    first_up,
    first_down,
    second_gate,
    second_up,
    second_down,
):
    weights, flips = [], []
    for w in (first_gate, first_up, second_gate, second_up, teacher_gate, teacher_up):
        flip = w.shape[1] % 128 != 0
        flips.append(flip)
        weights.append(w.T if flip else w)
    gathered, *rest = forward_call(mp, tokens, weights, tuple(flips))
    hidden, kept = rest[:3], rest[3:]
    target = jnp.dot(hidden[2], teacher_down, preferred_element_type=jnp.float32)
    diffs = (
        jnp.dot(hidden[0], first_down, preferred_element_type=jnp.float32) - target,
        jnp.dot(hidden[1], second_down, preferred_element_type=jnp.float32) - target,
    )
    counted = jnp.sum(lengths).astype(jnp.float32)
    mask = valid_rows(lengths, gathered.shape[0])
    scale = jnp.broadcast_to(2.0 * mask / counted, (mask.shape[0], 128))
    *made, loss = backward_call(diffs, scale, (first_down, second_down), kept)
    cots, grads_in = made[:2], made[2:]
    downs = [contract_rows(hidden[i], cots[i]).astype(jnp.bfloat16) for i in range(2)]
    outs = []
    for item, flip in zip(grads_in, flips):
        if flip:
            outs.append(contract_rows(item, gathered).astype(jnp.bfloat16).T)
        else:
            outs.append(contract_rows(gathered, item).astype(jnp.bfloat16))
    return outs[0], outs[1], downs[0], outs[2], outs[3], downs[1], loss[0:2, 0]


def per_device(
    tokens,
    lengths,
    teacher_gate,
    teacher_up,
    teacher_down,
    first_gate,
    first_up,
    first_down,
    second_gate,
    second_up,
    second_down,
):
    gathered = lax.all_gather(tokens, "mp", axis=0, tiled=True)
    total_rows = gathered.shape[0]

    def project(weight):
        return jnp.dot(gathered, weight, preferred_element_type=jnp.float32)

    partials = (
        project(teacher_gate),
        project(teacher_up),
        project(first_gate),
        project(first_up),
        project(second_gate),
        project(second_up),
    )
    values = lax.psum(
        (partials[0], partials[1], partials[2], partials[3], partials[4], partials[5]), "split"
    )
    hidden = (
        activate(values[0], values[1]),
        activate(values[2], values[3]),
        activate(values[4], values[5]),
    )
    target = jnp.dot(hidden[0], teacher_down, preferred_element_type=jnp.float32)
    diffs = (
        jnp.dot(hidden[1], first_down, preferred_element_type=jnp.float32) - target,
        jnp.dot(hidden[2], second_down, preferred_element_type=jnp.float32) - target,
    )
    counted = jnp.sum(lengths).astype(jnp.float32)
    summed = lax.psum((diffs[0], diffs[1]), "mp")
    mask = valid_rows(lengths, total_rows)
    partial_loss = (
        jnp.stack([jnp.sum(mask * summed[0] * summed[0]), jnp.sum(mask * summed[1] * summed[1])])
        / counted
    )
    losses = lax.psum(partial_loss, "split")
    cotangents = (
        (2.0 * mask * summed[0] / counted).astype(jnp.bfloat16),
        (2.0 * mask * summed[1] / counted).astype(jnp.bfloat16),
    )
    grad_first_down = contract_rows(hidden[1], cotangents[0]).astype(jnp.bfloat16)
    grad_second_down = contract_rows(hidden[2], cotangents[1]).astype(jnp.bfloat16)
    dims = (((1,), (1,)), ((), ()))
    backs = (
        lax.dot_general(cotangents[0], first_down, dims, preferred_element_type=jnp.float32),
        lax.dot_general(cotangents[1], second_down, dims, preferred_element_type=jnp.float32),
    )
    back_full = lax.psum((backs[0], backs[1]), "split")
    first_dg, first_du = hidden_grads(back_full[0], values[2], values[3])
    second_dg, second_du = hidden_grads(back_full[1], values[4], values[5])
    grads_in = (first_dg, first_du, second_dg, second_du)
    outputs = tuple((contract_rows(gathered, item).astype(jnp.bfloat16) for item in grads_in))
    return (
        outputs[0],
        outputs[1],
        grad_first_down,
        outputs[2],
        outputs[3],
        grad_second_down,
        losses,
    )


def run(mp, split, *args):
    rows = args[0].shape[0] * mp
    if split == 4 and mp == 4 and args[0].shape[0] % 16 == 0 and rows % 64 == 0:
        return per_device_kernels(mp, *args)
    return per_device(*args)


def solution(mesh):
    placed = (
        P(("parts", "mp"), "split"),
        P("parts"),
        P(("parts", "split"), "mp"),
        P(("parts", "split"), "mp"),
        P(("parts", "mp"), "split"),
        P(("parts", "split"), "mp"),
        P(("parts", "split"), "mp"),
        P(("parts", "mp"), "split"),
        P(("parts", "split"), "mp"),
        P(("parts", "split"), "mp"),
        P(("parts", "mp"), "split"),
    )
    return jax.shard_map(
        functools.partial(run, mesh.shape["mp"], mesh.shape["split"]),
        mesh=mesh,
        in_specs=placed,
        out_specs=(
            P(("parts", "split"), "mp"),
            P(("parts", "split"), "mp"),
            P(("parts", "mp"), "split"),
            P(("parts", "split"), "mp"),
            P(("parts", "split"), "mp"),
            P(("parts", "mp"), "split"),
            P("parts"),
        ),
        check_vma=False,
    )
```

profile of v0, /device:TPU:1, one launch (start us, length us, event | category | flops | bytes accessed | tf_op | source)
XLA Modules:
  0.0 173.9 jit_solution(6205232493686142911)
XLA Ops:
  0.6 66.7 %shard_map.162 = (bf16[192,1280]{1,0:T(8,128)(2,1)}, bf16[192,1728]{1,0:T(8,128)(2,1)}, bf16[192,1408]{1,0:T(8,128)(2,1)}, bf16[192,3456]{1,0:T(8,128)(2,1)}, f3...) custom-call(bf16[48,1280]{1,0:T(8,128)(2,1)} %refs_0_.1, ...), custom_call_target="tpu_custom_call" | custom-call | tf_op jit(solution)/shard_map/pallas_call | solution.py:267
  67.4 0.0 copy-start.1
  67.4 0.0 copy-start.3
  67.4 6.0 %fusion.1 = f32[192,1280]{1,0:T(8,128)S(1)} fusion(bf16[192,3456]{1,0:T(8,128)(2,1)} %get-tuple-element.24, bf16[3456,1280]{1,0:T(8,128)(2,1)} %param.15), kind=kOutput, calls=%fused_computation.18 | convolution fusion | flops 1698693120 | bytes 11157504 | tf_op jit(solution)/shard_map/dot_general | solution.py:414
  73.4 0.0 copy-start.2
  73.4 0.0 copy-start.4
  73.4 0.0 copy-done.1
  73.4 0.0 copy-done.3
  73.4 2.0 %convolution_subtract_fusion.1.refs_0_ = f32[192,1280]{1,0:T(8,128)} fusion(f32[192,1280]{1,0:T(8,128)S(1)} %fusion.1, bf16[192,1728]{1,0:T(8,128)(2,1)S(1)} %copy-done.3, bf16[1728,1280]{1,0:T(8,128)(2,1)S(1)} %copy-done.1), kind=kOutput, calls=%fused_computation.7 | convolution fusion | flops 849592320 | bytes 7053312 | tf_op jit(solution)/shard_map/dot_general | solution.py:416
  75.5 0.0 copy-start.10
  75.5 0.0 copy-done.2
  75.5 0.3 copy-done.4
  75.8 1.9 %convolution_subtract_fusion.refs_1_ = f32[192,1280]{1,0:T(8,128)} fusion(f32[192,1280]{1,0:T(8,128)S(1)} %fusion.1, bf16[192,1408]{1,0:T(8,128)(2,1)S(1)} %copy-done.4, bf16[1408,1280]{1,0:T(8,128)(2,1)S(1)} %copy-done.2), kind=kOutput, calls=%fused_computation.6 | convolution fusion | flops 692305920 | bytes 6111232 | tf_op jit(solution)/shard_map/dot_general | solution.py:417
  77.7 0.0 copy-done.10
  77.7 0.1 select_reduce_fusion
  77.8 0.6 reduce_sum.19
  79.1 0.7 broadcast_in_dim.23.refs_2_
  79.8 0.0 copy-start
  79.8 72.0 %shard_map.163 = (bf16[192,1280]{1,0:T(8,128)(2,1)}, bf16[192,1280]{1,0:T(8,128)(2,1)}, bf16[192,1728]{1,0:T(8,128)(2,1)}, bf16[192,1728]{1,0:T(8,128)(2,1)}, bf...) custom-call(f32[192,1280]{1,0:T(8,128)} %convolution_subtract_fusion.1.refs_0_, ...), custom_call_target="tpu_custom_call" | custom-call | tf_op jit(solution)/shard_map/pallas_call | solution.py:381
  151.9 0.0 copy-start.5
  151.9 0.0 copy-done
  151.9 4.6 %convolution_convert_fusion.5 = bf16[1280,1728]{0,1:T(8,128)(2,1)} fusion(bf16[192,1280]{1,0:T(8,128)(2,1)S(1)} %copy-done, bf16[192,1728]{1,0:T(8,128)(2,1)} %get-tuple-element.30), kind=kOutput, calls=%fused_computation.5 | convolution fusion | flops 851558400 | bytes 5578752 | tf_op jit(solution)/shard_map/dot_general | solution.py:20
  156.5 0.0 copy-start.8
  156.5 0.0 copy-done.5
  156.5 3.5 %convolution_convert_fusion.4 = bf16[1280,1728]{0,1:T(8,128)(2,1)} fusion(bf16[192,1280]{1,0:T(8,128)(2,1)S(1)} %copy-done, bf16[192,1728]{1,0:T(8,128)(2,1)S(1)} %copy-done.5), kind=kOutput, calls=%fused_computation.4 | convolution fusion | flops 851558400 | bytes 5578752 | tf_op jit(solution)/shard_map/dot_general | solution.py:20
  160.0 0.0 copy-start.7
  160.0 0.0 copy-done.8
  160.0 3.5 %convolution_convert_fusion.3 = bf16[1728,1280]{1,0:T(8,128)(2,1)} fusion(bf16[192,1728]{1,0:T(8,128)(2,1)S(1)} %copy-done.3, bf16[192,1280]{1,0:T(8,128)(2,1)S(1)} %copy-done.8), kind=kOutput, calls=%fused_computation.3 | convolution fusion | flops 851558400 | bytes 5578752 | tf_op jit(solution)/shard_map/dot_general | solution.py:20
  163.5 0.0 copy-start.6
  163.5 0.0 copy-done.7
  163.5 3.0 %convolution_convert_fusion.2 = bf16[1280,1408]{1,0:T(8,128)(2,1)} fusion(bf16[192,1280]{1,0:T(8,128)(2,1)S(1)} %copy-done, bf16[192,1408]{1,0:T(8,128)(2,1)S(1)} %copy-done.7), kind=kOutput, calls=%fused_computation.2 | convolution fusion | flops 693862400 | bytes 4636672 | tf_op jit(solution)/shard_map/dot_general | solution.py:20
  166.5 0.0 copy-start.9
  166.5 0.0 copy-done.6
  166.5 3.0 %convolution_convert_fusion.1 = bf16[1280,1408]{1,0:T(8,128)(2,1)} fusion(bf16[192,1280]{1,0:T(8,128)(2,1)S(1)} %copy-done, bf16[192,1408]{1,0:T(8,128)(2,1)S(1)} %copy-done.6), kind=kOutput, calls=%fused_computation.1 | convolution fusion | flops 693862400 | bytes 4636672 | tf_op jit(solution)/shard_map/dot_general | solution.py:20
  169.6 0.0 copy-done.9
  169.6 3.0 %convolution_convert_fusion = bf16[1408,1280]{1,0:T(8,128)(2,1)} fusion(bf16[192,1408]{1,0:T(8,128)(2,1)S(1)} %copy-done.4, bf16[192,1280]{1,0:T(8,128)(2,1)S(1)} %copy-done.9), kind=kOutput, calls=%fused_computation | convolution fusion | flops 693862400 | bytes 4636672 | tf_op jit(solution)/shard_map/dot_general | solution.py:20
  172.5 1.3 slice_reduce_fusion
  (2 shorter events, 0.0 us)
Async XLA Ops:
  67.4 6.1 %copy-start.1 = (bf16[1728,1280]{1,0:T(8,128)(2,1)S(1)}, bf16[1728,1280]{1,0:T(8,128)(2,1)}, u32[]{:S(2)}) copy-start(bf16[1728,1280]{1,0:T(8,128)(2,1)} %refs_3_.3) | copy-start | bytes 13271044
  67.4 6.1 %copy-start.3 = (bf16[192,1728]{1,0:T(8,128)(2,1)S(1)}, bf16[192,1728]{1,0:T(8,128)(2,1)}, u32[]{:S(2)}) copy-start(bf16[192,1728]{1,0:T(8,128)(2,1)} %get-tuple-element.23) | copy-start | bytes 1990660
  73.4 2.1 %copy-start.2 = (bf16[1408,1280]{1,0:T(8,128)(2,1)S(1)}, bf16[1408,1280]{1,0:T(8,128)(2,1)}, u32[]{:S(2)}) copy-start(bf16[1408,1280]{1,0:T(8,128)(2,1)} %refs_4_.3) | copy-start | bytes 10813444
  73.4 2.4 %copy-start.4 = (bf16[192,1408]{1,0:T(8,128)(2,1)S(1)}, bf16[192,1408]{1,0:T(8,128)(2,1)}, u32[]{:S(2)}) copy-start(bf16[192,1408]{1,0:T(8,128)(2,1)} %get-tuple-element.25) | copy-start | bytes 1622020
  75.5 2.2 %copy-start.10 = (s32[3]{0:T(128)S(1)}, s32[3]{0:T(128)}, u32[]{:S(2)}) copy-start(s32[3]{0:T(128)} %param.12) | copy-start | bytes 40
  79.8 72.1 %copy-start = (bf16[192,1280]{1,0:T(8,128)(2,1)S(1)}, bf16[192,1280]{1,0:T(8,128)(2,1)}, u32[]{:S(2)}) copy-start(bf16[192,1280]{1,0:T(8,128)(2,1)} %get-tuple-element.22) | copy-start | bytes 1474564
  151.9 4.6 %copy-start.5 = (bf16[192,1728]{1,0:T(8,128)(2,1)S(1)}, bf16[192,1728]{1,0:T(8,128)(2,1)}, u32[]{:S(2)}) copy-start(bf16[192,1728]{1,0:T(8,128)(2,1)} %get-tuple-element.31) | copy-start | bytes 1990660
  156.5 3.5 %copy-start.8 = (bf16[192,1280]{1,0:T(8,128)(2,1)S(1)}, bf16[192,1280]{1,0:T(8,128)(2,1)}, u32[]{:S(2)}) copy-start(bf16[192,1280]{1,0:T(8,128)(2,1)} %get-tuple-element.32) | copy-start | bytes 1474564
  160.0 3.5 %copy-start.7 = (bf16[192,1408]{1,0:T(8,128)(2,1)S(1)}, bf16[192,1408]{1,0:T(8,128)(2,1)}, u32[]{:S(2)}) copy-start(bf16[192,1408]{1,0:T(8,128)(2,1)} %get-tuple-element.33) | copy-start | bytes 1622020
  163.5 3.0 %copy-start.6 = (bf16[192,1408]{1,0:T(8,128)(2,1)S(1)}, bf16[192,1408]{1,0:T(8,128)(2,1)}, u32[]{:S(2)}) copy-start(bf16[192,1408]{1,0:T(8,128)(2,1)} %get-tuple-element.34) | copy-start | bytes 1622020
  166.5 3.1 %copy-start.9 = (bf16[192,1280]{1,0:T(8,128)(2,1)S(1)}, bf16[192,1280]{1,0:T(8,128)(2,1)}, u32[]{:S(2)}) copy-start(bf16[192,1280]{1,0:T(8,128)(2,1)} %get-tuple-element.35) | copy-start | bytes 1474564
where the time goes:
time: 174 us
  Pallas kernels  139 us (80%)
  matrix products  30.6 us (18%)
  local copies, waits for them, and re-layouts  2.37 us (1%)
    pallas_call x1, Pallas kernels, backward_call(): pl.pallas_call(backward_kernel, out_shape=outs, in_specs=[VMEM] * 3 + [AN...  72 us
    pallas_call x1, Pallas kernels, forward_call(): pl.pallas_call(functools.partial(forward_kernel, flips), out_shape=outs,...  66.7 us
    dot_general x6, matrix products, contract_rows(): lax.dot_general(left, right, (((0,), (0,)), ((), ())), preferred_element_...  20.6 us
    dot_general x1, matrix products, per_device_kernels(): jnp.dot(hidden[2], teacher_down, preferred_element_type=jnp.float32)  6 us

commit v1 on v0

v1 whole, which is shorter than its diff:
```python
import functools

import jax
import jax.numpy as jnp
from jax import lax
from jax.experimental import pallas as pl
from jax.experimental.pallas import tpu as pltpu
from jax.sharding import PartitionSpec as P

MESH = pl.DeviceIdType.MESH
VMEM = pl.BlockSpec(memory_space=pltpu.VMEM)
ANY = pl.BlockSpec(memory_space=pl.ANY)
TILE = 384
GRANT = 67043328

LEN = 64


def contract_rows(left, right):
    return lax.dot_general(
        left, right, (((0,), (0,)), ((), ())), preferred_element_type=jnp.float32
    )


def valid_rows(lengths, count):
    position = jnp.arange(count, dtype=jnp.int32)
    seq_ids = position // LEN
    within = position - seq_ids * LEN
    limit = jnp.sum(
        jnp.where(
            seq_ids[:, None] == jnp.arange(lengths.shape[0], dtype=jnp.int32)[None, :],
            lengths[None, :],
            0,
        ),
        axis=1,
    )
    return (within < limit).astype(jnp.float32)[:, None]


def activate(gate, up):
    return (jax.nn.silu(gate) * up).astype(jnp.bfloat16)


def hidden_grads(back, gate, up):
    sig = jax.nn.sigmoid(gate)
    dgate = (back * up * sig * (1.0 + gate * (1.0 - sig))).astype(jnp.bfloat16)
    dup = (back * gate * sig).astype(jnp.bfloat16)
    return (dgate, dup)


def view(spot):
    return spot[0].at[spot[1]] if isinstance(spot, tuple) else spot


class Move:
    def __init__(self, *args):
        self.args = args

    def build(self):
        src, dst, send, recv, at, device = self.args
        if device is None:
            return pltpu.make_async_copy(view(src), view(dst), recv.at[at])
        return pltpu.make_async_remote_copy(
            src_ref=view(src),
            dst_ref=view(dst),
            send_sem=send.at[at],
            recv_sem=recv.at[at],
            device_id=device,
            device_id_type=MESH,
        )

    def wait(self):
        self.build().wait()

    def wait_recv(self):
        self.build().wait_recv()

    def wait_send(self):
        self.build().wait_send()


class Links:
    def __init__(self, send, recv):
        self.send, self.recv, self.count, self.made = send, recv, 0, []

    def copy(self, src, dst, device=None):
        made = Move(src, dst, self.send, self.recv, self.count, device)
        self.count += 1
        made.build().start()
        self.made.append(made)
        return made

    def settle(self, made):
        made.wait_send()
        self.made.remove(made)

    def drain(self):
        for made in self.made:
            made.wait_send()


def greet(devices):
    barrier = pltpu.get_barrier_semaphore()
    for device in devices:
        pl.semaphore_signal(barrier, inc=1, device_id=device, device_id_type=MESH)
    pl.semaphore_wait(barrier, len(devices))


def cuts(width, pieces):
    if width % 128:
        return [(0, width)]
    lanes, made, start = width // 128, [], 0
    for i in range(pieces):
        size = (lanes * (i + 1) // pieces - lanes * i // pieces) * 128
        if size:
            made.append((start, size))
        start += size
    return made


def tiles(piece, body, tile=TILE):
    start, width = piece
    full = width // tile
    if full == 1:
        body(pl.ds(start, tile))
    elif full:

        @pl.loop(0, full)
        def _(i):
            body(pl.ds(pl.multiple_of(start + i * tile, 128), tile))

    if width % tile:
        body(pl.ds(start + full * tile, width % tile))


def four_places(axis):
    me = lax.axis_index(axis)
    chip, core = me // 2, me % 2
    sib = chip * 2 + (1 - core)
    far = (1 - chip) * 2 + core
    diag = (1 - chip) * 2 + (1 - core)
    return me, sib, far, diag


class Places:
    def __init__(self, axis, count):
        self.axis, self.count = axis, count
        self.me, self.sib, self.far, self.diag = self.ids = four_places(axis)
        self.rows = [rows_at(place, count) for place in self.ids]

    def to(self, k):
        return {self.axis: self.ids[k]}


def rows_at(block, count):
    return pl.ds(pl.multiple_of(block * count, 16), count)


def part(ref, piece, rows=slice(None)):
    return ref, (rows, pl.ds(*piece))


class Unit:
    def __init__(self, links, places, refs):
        self.links, self.places = links, places
        self.snd1, self.own, self.rcv1, self.snd2, self.rcv2 = refs
        self.half = self.own.shape[0] // 2
        self.width = self.own.shape[1]
        self.first, self.second = {}, {}

    def pass_on(self, piece):
        self.first[piece] = self.links.copy(
            part(self.snd1, piece), part(self.rcv1, piece), self.places.to(1)
        )

    def multiply(self, left, weight, flip, piece):
        pair = 2 * self.half

        def body(cols):
            if flip:
                right, dims = weight[cols, :], (((1,), (1,)), ((), ()))
            else:
                right, dims = weight[:, cols], (((1,), (0,)), ((), ()))
            out = lax.dot_general(left[...], right, dims, preferred_element_type=jnp.float32)
            self.snd1[:, cols] = out[:pair].astype(self.snd1.dtype)
            self.own[:, cols] = out[pair:]

        tiles(piece, body)
        self.pass_on(piece)

    def take(self, source, piece):
        me, sib, far, diag = self.places.rows
        half = self.half
        cols = pl.ds(*piece)
        for i, rows in enumerate((diag, sib)):
            self.snd1[i * half : (i + 1) * half, cols] = source[rows, cols].astype(self.snd1.dtype)
        for i, rows in enumerate((far, me)):
            self.own[i * half : (i + 1) * half, cols] = source[rows, cols]
        self.pass_on(piece)

    def forward(self, piece):
        self.first[piece].wait_recv()
        half = self.half

        def body(cols):
            both = self.own[:half, cols] + self.rcv1[:half, cols].astype(jnp.float32)
            self.snd2[:, cols] = both.astype(jnp.bfloat16)

        tiles(piece, body)
        self.second[piece] = self.links.copy(
            part(self.snd2, piece), part(self.rcv2, piece), self.places.to(2)
        )

    def ready(self, piece):
        self.second[piece].wait_recv()

    def value(self, cols):
        half = self.half
        return (
            self.own[half:, cols]
            + self.rcv1[half:, cols].astype(jnp.float32)
            + self.rcv2[:, cols].astype(jnp.float32)
        )

    def settle(self):
        for made in (*self.first.values(), *self.second.values()):
            self.links.settle(made)


def unit_scratch(rows, width, kind=jnp.float32):
    half, pair = rows // 4, rows // 2
    return [
        pltpu.VMEM((pair, width), kind),
        pltpu.VMEM((pair, width), jnp.float32),
        pltpu.VMEM((pair, width), kind),
        pltpu.VMEM((half, width), jnp.bfloat16),
        pltpu.VMEM((half, width), jnp.bfloat16),
    ]


class Spread:
    def __init__(self, links, ref, places, piece=None, source=None):
        self.links, self.places = links, places
        piece = (0, ref.shape[1]) if piece is None else piece
        mine = part(ref, piece, places.rows[0])
        self.theirs = part(ref, piece, places.rows[2])
        source = mine if source is None else source
        self.out = links.copy(source, mine, places.to(2))
        self.side = links.copy(source, mine, places.to(1))

    def relay(self):
        self.out.wait_recv()
        self.last = self.links.copy(self.theirs, self.theirs, self.places.to(1))

    def finish(self):
        self.side.wait_recv()
        self.last.wait_recv()


def arrange(dst, src, places):
    me, sib, far, diag = places.rows
    count = places.count
    for i, rows in enumerate((diag, sib, far, me)):
        dst[i * count : (i + 1) * count, :] = src[rows, :]


def row_scale(scale, lengths):
    position = lax.broadcasted_iota(jnp.int32, scale.shape, 0)
    seq_ids = position // LEN
    within = position - seq_ids * LEN
    limit, counted = jnp.zeros(scale.shape, jnp.int32), 0
    for i in range(lengths.shape[0]):
        length = lengths[i]
        limit = jnp.where(seq_ids == i, length, limit)
        counted = counted + length
    whole = jnp.full(scale.shape, counted, jnp.int32).astype(jnp.float32)
    scale[...] = jnp.where(within < limit, 2.0 / whole, 0.0)


def layer_kernel(flips, *refs):
    refs = iter(refs)

    def take(n):
        return [next(refs) for _ in range(n)]

    (tok, lengths), weights, downs = take(2), take(6), take(3)
    kept_out, loss = take(9), take(1)[0]
    gathered, xp, xq = take(3)
    hidden, grads, cots = take(3), take(4), take(2)
    target, diff, scale, part_sums, marked = take(5)
    unit_refs = [take(5) for _ in range(6)]
    ring_refs = [take(5) for _ in range(2)]
    send, recv, wsem, dsem, osem = take(5)

    links, loads, stores = Links(send, recv), Links(None, wsem), Links(None, osem)
    places, ring = Places("split", tok.shape[0]), Places("mp", tok.shape[0])
    mine, turn = places.rows[0], ring.rows[0]
    units = [Unit(links, places, r) for r in unit_refs]
    rings = [Unit(links, ring, r) for r in ring_refs]
    layers = ((2, 3), (0, 1), (1, 2))
    pieces = {layer: cuts(units[2 * layer].width, n) for layer, n in layers}
    out = []

    def project(*wbuf):
        waits = {}
        for layer, _ in layers:
            for piece in pieces[layer]:
                for i in (2 * layer, 2 * layer + 1):
                    src, dst = weights[i], wbuf[i]
                    if piece != (0, units[i].width):
                        at = (pl.ds(*piece), slice(None))
                        at = at if flips[i] else at[::-1]
                        src, dst = (src, at), (dst, at)
                    waits[i, piece] = loads.copy(src, dst)
        row_scale(scale, lengths)
        greet([spot.to(k) for spot in (places, ring) for k in (1, 2, 3)])
        moves = Spread(links, gathered, ring, source=tok)
        gathered[turn, :] = tok[...]
        moves.relay()
        moves.finish()
        out.append(stores.copy(gathered, kept_out[0]))
        arrange(xp, gathered, places)
        behind = None
        for layer, _ in layers:
            for piece in pieces[layer]:
                for i in (2 * layer, 2 * layer + 1):
                    waits[i, piece].wait()
                    units[i].multiply(xp, wbuf[i], flips[i], piece)
                    if behind is not None:
                        units[behind[0]].forward(behind[1])
                    behind = (i, piece) if layer != 1 else None

    pl.run_scoped(project, *[pltpu.VMEM(w.shape, jnp.bfloat16) for w in weights])

    def rest(*dbuf):
        waits = {}
        drops = Links(None, dsem)
        for layer, _ in layers:
            for piece in pieces[layer]:
                rows = pl.ds(*piece)
                src, dst = (downs[layer], rows), (dbuf[layer], rows)
                waits[layer, piece] = drops.copy(src, dst)
        spreads = {}

        def activate(layer, piece):
            gate, up = units[2 * layer], units[2 * layer + 1]
            gate.ready(piece)
            up.ready(piece)

            def body(cols):
                g, u = gate.value(cols), up.value(cols)
                hidden[layer][mine, cols] = (g * jax.nn.sigmoid(g) * u).astype(
                    jnp.bfloat16
                )
                if layer < 2:
                    gate.own[gate.half :, cols] = g
                    up.own[up.half :, cols] = u

            tiles(piece, body)
            spreads[layer, piece] = Spread(links, hidden[layer], places, piece)

        wide = (0, target.shape[1])

        def project_down(layer, piece, first, dst, sign):
            spreads[layer, piece].finish()
            waits[layer, piece].wait()
            rows = pl.ds(*piece)

            def body(cols):
                out = jnp.dot(
                    hidden[layer][:, rows],
                    dbuf[layer][rows, cols],
                    preferred_element_type=jnp.float32,
                )
                if first is None:
                    dst[:, cols] += out
                elif sign:
                    dst[:, cols] = out
                else:
                    dst[:, cols] = out - first[:, cols]

            tiles(wide, body, 256)

        halves = cuts(target.shape[1], 2)
        for piece in pieces[2]:
            activate(2, piece)
        for piece in pieces[0]:
            activate(0, piece)
        for piece in pieces[1]:
            for i in (2, 3):
                units[i].forward(piece)
        for piece in pieces[2]:
            spreads[2, piece].relay()
        for n, piece in enumerate(pieces[2]):
            project_down(2, piece, None if n else target, target, n == 0)
        for piece in pieces[0]:
            spreads[0, piece].relay()
        for n, piece in enumerate(pieces[0]):
            project_down(0, piece, None if n else target, diff, False)
        out.append(stores.copy(hidden[0], kept_out[1]))
        for half in halves:
            rings[0].take(diff, half)
        for piece in pieces[1]:
            activate(1, piece)
        for half in halves:
            rings[0].forward(half)
        for piece in pieces[1]:
            spreads[1, piece].relay()
        for n, piece in enumerate(pieces[1]):
            project_down(1, piece, None if n else target, target, False)
        out.append(stores.copy(hidden[1], kept_out[2]))
        for half in halves:
            rings[1].take(target, half)

        factor = scale[turn, 0:1]
        turns, sums = [], []

        def cotangent(i):
            total_sum = 0.0
            for half in halves:
                rings[i].ready(half)
                cols = pl.ds(*half)
                total = rings[i].value(cols)
                scaled = factor * total
                cots[i][turn, cols] = scaled.astype(jnp.bfloat16)
                total_sum = total_sum + jnp.sum(scaled * total, keepdims=True)
            turns.append(Spread(links, cots[i], ring))
            sums.append(0.5 * total_sum)

        back = []
        for i in range(2):
            gate, up = units[2 * i], units[2 * i + 1]
            back.append(
                Unit(links, places, (gate.snd1, up.snd1, gate.rcv1, gate.snd2, gate.rcv2))
            )
            gate.settle()
            up.settle()
        gates = {}

        def differentiate(i):
            whole = (0, back[i].width)
            back[i].ready(whole)
            gate, up = units[2 * i], units[2 * i + 1]
            half = gate.half

            def body(cols):
                b = back[i].value(cols)
                g, u = gate.own[half:, cols], up.own[half:, cols]
                sig = jax.nn.sigmoid(g)
                dgate = b * u * sig * (1.0 + g * (1.0 - sig))
                grads[2 * i][mine, cols] = dgate.astype(jnp.bfloat16)
                grads[2 * i + 1][mine, cols] = (b * g * sig).astype(jnp.bfloat16)

            tiles(whole, body)
            gates[i] = [Spread(links, grads[2 * i + j], places) for j in range(2)]

        def back_project(i, left):
            turns[i].finish()
            out.append(stores.copy(cots[i], kept_out[3 + i]))
            arrange(left, cots[i], places)
            back[i].multiply(left, dbuf[i], True, (0, back[i].width))

        cotangent(0)
        for half in halves:
            rings[1].forward(half)
        turns[0].relay()
        cotangent(1)
        row = lax.broadcasted_iota(jnp.int32, part_sums.shape[1:], 0)
        part_sums[0] = jnp.where(row == 0, sums[0], sums[1])
        parts = [
            links.copy((part_sums, 0), (part_sums, k), ring.to(k)) for k in (1, 2, 3)
        ]
        back_project(0, xp)
        back[0].forward((0, back[0].width))
        turns[1].relay()
        differentiate(0)
        back_project(1, xq)
        back[1].forward((0, back[1].width))
        for move in parts:
            move.wait_recv()
        marked[0] = part_sums[0] + part_sums[1] + part_sums[2] + part_sums[3]
        marks = [
            links.copy((marked, 0), (marked, k), places.to(k)) for k in (1, 2, 3)
        ]
        for spread in gates[0]:
            spread.relay()
        differentiate(1)
        for mark in marks:
            mark.wait_recv()
        loss[...] = marked[0] + marked[1] + marked[2] + marked[3]
        for j, spread in enumerate(gates[0]):
            spread.finish()
            out.append(stores.copy(grads[j], kept_out[5 + j]))
        for spread in gates[1]:
            spread.relay()
        for j, spread in enumerate(gates[1]):
            spread.finish()
            out.append(stores.copy(grads[2 + j], kept_out[7 + j]))

        for made in out:
            made.wait()
        links.drain()

    pl.run_scoped(rest, *[pltpu.VMEM(d.shape, jnp.bfloat16) for d in downs])


def layer_call(mp, tokens, lengths, weights, downs, flips):
    block, depth = tokens.shape
    rows = block * mp
    widths = [d.shape[0] for d in downs]
    shape, bf16, f32 = jax.ShapeDtypeStruct, jnp.bfloat16, jnp.float32
    outs = [shape((rows, depth), bf16)]
    outs += [shape((rows, widths[i]), bf16) for i in range(2)]
    outs += [shape((rows, depth), bf16)] * 2
    outs += [shape((rows, widths[i // 2]), bf16) for i in range(4)]
    outs.append(shape((8, 128), f32))
    scratch = [pltpu.VMEM((rows, depth), bf16)] * 3
    scratch += [pltpu.VMEM((rows, w), bf16) for w in widths]
    scratch += [pltpu.VMEM((rows, widths[i // 2]), bf16) for i in range(4)]
    scratch += [pltpu.VMEM((rows, depth), bf16)] * 2
    scratch += [pltpu.VMEM((rows, depth), f32)] * 2
    scratch += [pltpu.VMEM((rows, 128), f32)]
    scratch += [pltpu.VMEM((4, 8, 128), f32)] * 2
    for i in range(6):
        scratch += unit_scratch(rows, widths[i // 2])
    for _ in range(2):
        scratch += unit_scratch(rows, depth, bf16)
    copies = 120
    scratch += [pltpu.SemaphoreType.DMA((copies,))] * 2
    scratch += [pltpu.SemaphoreType.DMA((16,))] * 3
    return pl.pallas_call(
        functools.partial(layer_kernel, flips),
        out_shape=outs,
        in_specs=[VMEM, pl.BlockSpec(memory_space=pltpu.SMEM)] + [ANY] * 9,
        out_specs=[ANY] * 9 + [VMEM],
        scratch_shapes=scratch,
        compiler_params=pltpu.CompilerParams(
            collective_id=0, has_side_effects=True, vmem_limit_bytes=GRANT
        ),
    )(tokens, lengths, *weights, *downs)


def per_device_kernels(
    mp,
    tokens,
    lengths,
    teacher_gate,
    teacher_up,
    teacher_down,
    first_gate,
    first_up,
    first_down,
    second_gate,
    second_up,
    second_down,
):
    weights, flips = [], []
    for w in (first_gate, first_up, second_gate, second_up, teacher_gate, teacher_up):
        flip = w.shape[1] % 128 != 0
        flips.append(flip)
        weights.append(w.T if flip else w)
    gathered, *rest = layer_call(
        mp, tokens, lengths, weights, (first_down, second_down, teacher_down), tuple(flips)
    )
    hidden, cots, grads_in, loss = rest[:2], rest[2:4], rest[4:8], rest[8]
    downs = [contract_rows(hidden[i], cots[i]).astype(jnp.bfloat16) for i in range(2)]
    outs = []
    for item, flip in zip(grads_in, flips):
        if flip:
            outs.append(contract_rows(item, gathered).astype(jnp.bfloat16).T)
        else:
            outs.append(contract_rows(gathered, item).astype(jnp.bfloat16))
    return outs[0], outs[1], downs[0], outs[2], outs[3], downs[1], loss[0:2, 0]


def per_device(
    tokens,
    lengths,
    teacher_gate,
    teacher_up,
    teacher_down,
    first_gate,
    first_up,
    first_down,
    second_gate,
    second_up,
    second_down,
):
    gathered = lax.all_gather(tokens, "mp", axis=0, tiled=True)
    total_rows = gathered.shape[0]

    def project(weight):
        return jnp.dot(gathered, weight, preferred_element_type=jnp.float32)

    partials = (
        project(teacher_gate),
        project(teacher_up),
        project(first_gate),
        project(first_up),
        project(second_gate),
        project(second_up),
    )
    values = lax.psum(
        (partials[0], partials[1], partials[2], partials[3], partials[4], partials[5]), "split"
    )
    hidden = (
        activate(values[0], values[1]),
        activate(values[2], values[3]),
        activate(values[4], values[5]),
    )
    target = jnp.dot(hidden[0], teacher_down, preferred_element_type=jnp.float32)
    diffs = (
        jnp.dot(hidden[1], first_down, preferred_element_type=jnp.float32) - target,
        jnp.dot(hidden[2], second_down, preferred_element_type=jnp.float32) - target,
    )
    counted = jnp.sum(lengths).astype(jnp.float32)
    summed = lax.psum((diffs[0], diffs[1]), "mp")
    mask = valid_rows(lengths, total_rows)
    partial_loss = (
        jnp.stack([jnp.sum(mask * summed[0] * summed[0]), jnp.sum(mask * summed[1] * summed[1])])
        / counted
    )
    losses = lax.psum(partial_loss, "split")
    cotangents = (
        (2.0 * mask * summed[0] / counted).astype(jnp.bfloat16),
        (2.0 * mask * summed[1] / counted).astype(jnp.bfloat16),
    )
    grad_first_down = contract_rows(hidden[1], cotangents[0]).astype(jnp.bfloat16)
    grad_second_down = contract_rows(hidden[2], cotangents[1]).astype(jnp.bfloat16)
    dims = (((1,), (1,)), ((), ()))
    backs = (
        lax.dot_general(cotangents[0], first_down, dims, preferred_element_type=jnp.float32),
        lax.dot_general(cotangents[1], second_down, dims, preferred_element_type=jnp.float32),
    )
    back_full = lax.psum((backs[0], backs[1]), "split")
    first_dg, first_du = hidden_grads(back_full[0], values[2], values[3])
    second_dg, second_du = hidden_grads(back_full[1], values[4], values[5])
    grads_in = (first_dg, first_du, second_dg, second_du)
    outputs = tuple((contract_rows(gathered, item).astype(jnp.bfloat16) for item in grads_in))
    return (
        outputs[0],
        outputs[1],
        grad_first_down,
        outputs[2],
        outputs[3],
        grad_second_down,
        losses,
    )


def run(mp, split, *args):
    rows = args[0].shape[0] * mp
    if split == 4 and mp == 4 and args[0].shape[0] % 16 == 0 and rows % 64 == 0:
        return per_device_kernels(mp, *args)
    return per_device(*args)


def solution(mesh):
    placed = (
        P(("parts", "mp"), "split"),
        P("parts"),
        P(("parts", "split"), "mp"),
        P(("parts", "split"), "mp"),
        P(("parts", "mp"), "split"),
        P(("parts", "split"), "mp"),
        P(("parts", "split"), "mp"),
        P(("parts", "mp"), "split"),
        P(("parts", "split"), "mp"),
        P(("parts", "split"), "mp"),
        P(("parts", "mp"), "split"),
    )
    return jax.shard_map(
        functools.partial(run, mesh.shape["mp"], mesh.shape["split"]),
        mesh=mesh,
        in_specs=placed,
        out_specs=(
            P(("parts", "split"), "mp"),
            P(("parts", "split"), "mp"),
            P(("parts", "mp"), "split"),
            P(("parts", "split"), "mp"),
            P(("parts", "split"), "mp"),
            P(("parts", "mp"), "split"),
            P("parts"),
        ),
        check_vma=False,
    )
```

time: 174 us -> 145 us (0.83); the launches traced: 174 us -> 143 us
  Pallas kernels: 139 us -> 120 us
  matrix products: 30.6 us -> 20.8 us
    pallas_call x2 -> x1, Pallas kernels: 139 us -> 120 us  [layer_call(): pl.pallas_call(functools.partial(layer_kernel, flips), out_shape=outs, in...]
    dot_general x3 -> x0, matrix products: 9.97 us -> none  [the longest x1 6 us: per_device_kernels(): jnp.dot(hidden[2], teacher_down, preferred_element_type=jnp.float32)]
where the time goes in v1:
time: 145 us; the launch traced here: 143 us
  Pallas kernels  120 us (83%)
  matrix products  20.8 us (14%)
    pallas_call x1, Pallas kernels, layer_call(): pl.pallas_call(functools.partial(layer_kernel, flips), out_shape=outs, in...  120 us
    dot_general x6, matrix products, contract_rows(): lax.dot_general(left, right, (((0,), (0,)), ((), ())), preferred_element_...  20.8 us

profile of v1, /device:TPU:1, one launch (start us, length us, event | category | flops | bytes accessed | tf_op | source)
XLA Modules:
  0.0 142.8 jit_solution(4505629816718537632)
XLA Ops:
  0.6 120.0 %shard_map.162 = (bf16[192,1280]{1,0:T(8,128)(2,1)}, bf16[192,1728]{1,0:T(8,128)(2,1)}, bf16[192,1408]{1,0:T(8,128)(2,1)}, bf16[192,1280]{1,0:T(8,128)(2,1)}, bf...) custom-call(bf16[48,1280]{1,0:T(8,128)(2,1)} %refs_0_.1, ...), custom_call_target="tpu_custom_call" | custom-call | tf_op jit(solution)/shard_map/pallas_call | solution.py:531
  120.6 0.0 copy-start
  120.6 0.0 copy-start.5
  120.6 4.8 %convolution_convert_fusion.4 = bf16[1280,1728]{0,1:T(8,128)(2,1)} fusion(bf16[192,1280]{1,0:T(8,128)(2,1)} %get-tuple-element.17, bf16[192,1728]{1,0:T(8,128)(2,1)} %get-tuple-element.19), kind=kOutput, calls=%fused_computation.4 | convolution fusion | flops 851558400 | bytes 5578752 | tf_op jit(solution)/shard_map/dot_general | solution.py:20
  125.4 0.0 copy-start.4
  125.4 0.0 copy-done
  125.4 0.0 copy-done.5
  125.4 3.0 %convolution_convert_fusion.1 = bf16[1280,1408]{1,0:T(8,128)(2,1)} fusion(bf16[192,1280]{1,0:T(8,128)(2,1)S(1)} %copy-done, bf16[192,1408]{1,0:T(8,128)(2,1)S(1)} %copy-done.5), kind=kOutput, calls=%fused_computation.1 | convolution fusion | flops 693862400 | bytes 4636672 | tf_op jit(solution)/shard_map/dot_general | solution.py:20
  128.5 0.0 copy-start.3
  128.5 0.0 copy-done.4
  128.5 3.0 %convolution_convert_fusion.2 = bf16[1280,1408]{1,0:T(8,128)(2,1)} fusion(bf16[192,1280]{1,0:T(8,128)(2,1)S(1)} %copy-done, bf16[192,1408]{1,0:T(8,128)(2,1)S(1)} %copy-done.4), kind=kOutput, calls=%fused_computation.2 | convolution fusion | flops 693862400 | bytes 4636672 | tf_op jit(solution)/shard_map/dot_general | solution.py:20
  131.5 0.0 copy-start.2
  131.5 0.0 copy-start.6
  131.5 0.0 copy-done.3
  131.5 3.5 %convolution_convert_fusion.5 = bf16[1280,1728]{0,1:T(8,128)(2,1)} fusion(bf16[192,1280]{1,0:T(8,128)(2,1)S(1)} %copy-done, bf16[192,1728]{1,0:T(8,128)(2,1)S(1)} %copy-done.3), kind=kOutput, calls=%fused_computation.5 | convolution fusion | flops 851558400 | bytes 5578752 | tf_op jit(solution)/shard_map/dot_general | solution.py:20
  135.0 0.0 copy-start.1
  135.0 0.0 copy-start.7
  135.0 0.0 copy-done.2
  135.0 0.0 copy-done.6
  135.0 3.5 %convolution_convert_fusion.3 = bf16[1728,1280]{1,0:T(8,128)(2,1)} fusion(bf16[192,1728]{1,0:T(8,128)(2,1)S(1)} %copy-done.2, bf16[192,1280]{1,0:T(8,128)(2,1)S(1)} %copy-done.6), kind=kOutput, calls=%fused_computation.3 | convolution fusion | flops 851558400 | bytes 5578752 | tf_op jit(solution)/shard_map/dot_general | solution.py:20
  138.5 0.0 copy-done.1
  138.5 0.0 copy-done.7
  138.5 3.0 %convolution_convert_fusion = bf16[1408,1280]{1,0:T(8,128)(2,1)} fusion(bf16[192,1408]{1,0:T(8,128)(2,1)S(1)} %copy-done.1, bf16[192,1280]{1,0:T(8,128)(2,1)S(1)} %copy-done.7), kind=kOutput, calls=%fused_computation | convolution fusion | flops 693862400 | bytes 4636672 | tf_op jit(solution)/shard_map/dot_general | solution.py:20
  141.5 1.3 slice_reduce_fusion
Async XLA Ops:
  120.6 4.8 %copy-start = (bf16[192,1280]{1,0:T(8,128)(2,1)S(1)}, bf16[192,1280]{1,0:T(8,128)(2,1)}, u32[]{:S(2)}) copy-start(bf16[192,1280]{1,0:T(8,128)(2,1)} %get-tuple-element.17) | copy-start | bytes 1474564
  120.6 4.8 %copy-start.5 = (bf16[192,1408]{1,0:T(8,128)(2,1)S(1)}, bf16[192,1408]{1,0:T(8,128)(2,1)}, u32[]{:S(2)}) copy-start(bf16[192,1408]{1,0:T(8,128)(2,1)} %get-tuple-element.23) | copy-start | bytes 1622020
  125.4 3.1 %copy-start.4 = (bf16[192,1408]{1,0:T(8,128)(2,1)S(1)}, bf16[192,1408]{1,0:T(8,128)(2,1)}, u32[]{:S(2)}) copy-start(bf16[192,1408]{1,0:T(8,128)(2,1)} %get-tuple-element.22) | copy-start | bytes 1622020
  128.5 3.0 %copy-start.3 = (bf16[192,1728]{1,0:T(8,128)(2,1)S(1)}, bf16[192,1728]{1,0:T(8,128)(2,1)}, u32[]{:S(2)}) copy-start(bf16[192,1728]{1,0:T(8,128)(2,1)} %get-tuple-element.18) | copy-start | bytes 1990660
  131.5 3.5 %copy-start.2 = (bf16[192,1728]{1,0:T(8,128)(2,1)S(1)}, bf16[192,1728]{1,0:T(8,128)(2,1)}, u32[]{:S(2)}) copy-start(bf16[192,1728]{1,0:T(8,128)(2,1)} %get-tuple-element.20) | copy-start | bytes 1990660
  131.5 3.5 %copy-start.6 = (bf16[192,1280]{1,0:T(8,128)(2,1)S(1)}, bf16[192,1280]{1,0:T(8,128)(2,1)}, u32[]{:S(2)}) copy-start(bf16[192,1280]{1,0:T(8,128)(2,1)} %get-tuple-element.21) | copy-start | bytes 1474564
  135.0 3.5 %copy-start.1 = (bf16[192,1408]{1,0:T(8,128)(2,1)S(1)}, bf16[192,1408]{1,0:T(8,128)(2,1)}, u32[]{:S(2)}) copy-start(bf16[192,1408]{1,0:T(8,128)(2,1)} %get-tuple-element.24) | copy-start | bytes 1622020
  135.0 3.5 %copy-start.7 = (bf16[192,1280]{1,0:T(8,128)(2,1)S(1)}, bf16[192,1280]{1,0:T(8,128)(2,1)}, u32[]{:S(2)}) copy-start(bf16[192,1280]{1,0:T(8,128)(2,1)} %get-tuple-element.25) | copy-start | bytes 1474564

commit v2 on v1

--- a/solution.py
+++ b/solution.py
@@ -540,6 +540,54 @@
     )(tokens, lengths, *weights, *downs)
 
 
+def gradient_kernel(jobs, *refs):
+    refs = iter(refs)
+
+    def take(n):
+        return [next(refs) for _ in range(n)]
+
+    sources, loss, outs, losses = take(9), take(1)[0], take(len(jobs)), take(1)[0]
+    held, made = take(9), take(len(jobs))
+    isem, osem = take(2)
+    order = list(dict.fromkeys(i for job in jobs for i in job))
+    loads = {i: pltpu.make_async_copy(sources[i], held[i], isem.at[i]) for i in order}
+    for i in order:
+        loads[i].start()
+    for i in range(losses.shape[0]):
+        losses[i] = loss[i, 0]
+    for j, job in enumerate(jobs):
+        for i in job:
+            if i in loads:
+                loads.pop(i).wait()
+        left, right, dst = held[job[0]], held[job[1]], made[j]
+        height, width = dst.shape
+        step = -(-height // 256) * 128
+        for start in range(0, height, step):
+            rows = pl.ds(start, min(step, height - start))
+            for at in range(0, width, 256):
+                cols = pl.ds(at, min(256, width - at))
+                dst[rows, cols] = contract_rows(left[:, rows], right[:, cols]).astype(dst.dtype)
+            pltpu.make_async_copy(dst.at[rows], outs[j].at[rows], osem.at[j]).start()
+    for j in range(len(jobs)):
+        pltpu.make_async_copy(made[j], outs[j], osem.at[j]).wait()
+
+
+def gradient_call(arrays, loss, jobs, students):
+    shape = jax.ShapeDtypeStruct
+    outs = [shape((arrays[a].shape[1], arrays[b].shape[1]), jnp.bfloat16) for a, b in jobs]
+    smem = pl.BlockSpec(memory_space=pltpu.SMEM)
+    scratch = [pltpu.VMEM(item.shape, item.dtype) for item in (*arrays, *outs)]
+    scratch += [pltpu.SemaphoreType.DMA((len(arrays),)), pltpu.SemaphoreType.DMA((len(jobs),))]
+    return pl.pallas_call(
+        functools.partial(gradient_kernel, jobs),
+        out_shape=outs + [shape((students,), jnp.float32)],
+        in_specs=[ANY] * len(arrays) + [smem],
+        out_specs=[ANY] * len(jobs) + [smem],
+        scratch_shapes=scratch,
+        compiler_params=pltpu.CompilerParams(vmem_limit_bytes=GRANT),
+    )(*arrays, loss)
+
+
 def per_device_kernels(
     mp,
     tokens,
@@ -559,18 +607,14 @@
         flip = w.shape[1] % 128 != 0
         flips.append(flip)
         weights.append(w.T if flip else w)
-    gathered, *rest = layer_call(
+    *arrays, loss = layer_call(
         mp, tokens, lengths, weights, (first_down, second_down, teacher_down), tuple(flips)
     )
-    hidden, cots, grads_in, loss = rest[:2], rest[2:4], rest[4:8], rest[8]
-    downs = [contract_rows(hidden[i], cots[i]).astype(jnp.bfloat16) for i in range(2)]
-    outs = []
-    for item, flip in zip(grads_in, flips):
-        if flip:
-            outs.append(contract_rows(item, gathered).astype(jnp.bfloat16).T)
-        else:
-            outs.append(contract_rows(gathered, item).astype(jnp.bfloat16))
-    return outs[0], outs[1], downs[0], outs[2], outs[3], downs[1], loss[0:2, 0]
+    jobs = [(1, 3), (2, 4)]
+    jobs += [(5 + i, 0) if flips[i] else (0, 5 + i) for i in range(4)]
+    made = gradient_call(arrays, loss, tuple(jobs), 2)
+    ins = [out.T if flip else out for out, flip in zip(made[2:6], flips)]
+    return ins[0], ins[1], made[0], ins[2], ins[3], made[1], made[6]
 
 
 def per_device(

time: 145 us -> 135 us (0.931)
  matrix products: 20.8 us -> 0 us
  Pallas kernels: 120 us -> 132 us
    dot_general x6 -> x0, matrix products: 20.8 us -> none  [contract_rows(): lax.dot_general(left, right, (((0,), (0,)), ((), ())), preferred_element_...]
    pallas_call x0 -> x1, Pallas kernels: none -> 12 us  [gradient_call(): pl.pallas_call(functools.partial(gradient_kernel, jobs), out_shape=outs +...]
where the time goes in v2:
time: 135 us; the launch traced here: 133 us
  Pallas kernels  132 us (98%)
    pallas_call x1, Pallas kernels, layer_call(): pl.pallas_call(functools.partial(layer_kernel, flips), out_shape=outs, in...  120 us
    pallas_call x1, Pallas kernels, gradient_call(): pl.pallas_call(functools.partial(gradient_kernel, jobs), out_shape=outs +...  12 us

profile of v2, /device:TPU:1, one launch (start us, length us, event | category | flops | bytes accessed | tf_op | source)
XLA Modules:
  0.0 133.1 jit_solution(11718970996148726490)
XLA Ops:
  0.6 120.3 %shard_map.162 = (bf16[192,1280]{1,0:T(8,128)(2,1)}, bf16[192,1728]{1,0:T(8,128)(2,1)}, bf16[192,1408]{1,0:T(8,128)(2,1)}, bf16[192,1280]{1,0:T(8,128)(2,1)}, bf...) custom-call(bf16[48,1280]{1,0:T(8,128)(2,1)} %refs_0_.1, ...), custom_call_target="tpu_custom_call" | custom-call | tf_op jit(solution)/shard_map/pallas_call | solution.py:531
  121.0 12.0 %shard_map.163 = (bf16[1728,1280]{1,0:T(8,128)(2,1)}, bf16[1408,1280]{1,0:T(8,128)(2,1)}, bf16[1728,1280]{1,0:T(8,128)(2,1)}, bf16[1728,1280]{1,0:T(8,128)(2,1)}...) custom-call(bf16[192,1280]{1,0:T(8,128)(2,1)} %get-tuple-element.24.refs_0_, ...), custom_call_target="tpu_custom_call" | custom-call | tf_op jit(solution)/shard_map/pallas_call | solution.py:581

commit v3 on v2

--- a/solution.py
+++ b/solution.py
@@ -106,15 +106,16 @@
     pl.semaphore_wait(barrier, len(devices))
 
 
-def cuts(width, pieces):
+def cuts(width, shares):
     if width % 128:
         return [(0, width)]
-    lanes, made, start = width // 128, [], 0
-    for i in range(pieces):
-        size = (lanes * (i + 1) // pieces - lanes * i // pieces) * 128
-        if size:
-            made.append((start, size))
-        start += size
+    lanes, whole, made, taken, start = width // 128, sum(shares), [], 0, 0
+    for share in shares:
+        taken += share
+        end = lanes * taken // whole * 128
+        if end > start:
+            made.append((start, end - start))
+        start = end
     return made
 
 
@@ -225,6 +226,37 @@
     def settle(self):
         for made in (*self.first.values(), *self.second.values()):
             self.links.settle(made)
+
+
+class Exchange(Unit):
+    def __init__(self, links, places, refs):
+        super().__init__(links, places, (*refs[:3], None, None))
+        self.snd2, self.rcv2 = refs[3], refs[4]
+
+    def forward(self, piece):
+        self.first[piece].wait_recv()
+        half = self.half
+
+        def body(cols):
+            for k in range(2):
+                rows = slice(k * half, (k + 1) * half)
+                both = self.own[rows, cols] + self.rcv1[rows, cols]
+                self.own[rows, cols] = both
+                self.snd2[k][:, cols] = both.astype(jnp.bfloat16)
+
+        tiles(piece, body)
+        self.second[piece] = [
+            self.links.copy(part(self.snd2[k], piece), part(self.rcv2[1 - k], piece), self.places.to(2))
+            for k in range(2)
+        ]
+
+    def ready(self, piece):
+        for made in self.second[piece]:
+            made.wait_recv()
+
+    def value(self, k, cols):
+        rows = slice(k * self.half, (k + 1) * self.half)
+        return self.own[rows, cols] + self.rcv2[k][:, cols].astype(jnp.float32)
 
 
 def unit_scratch(rows, width, kind=jnp.float32):
@@ -287,6 +319,7 @@
     kept_out, loss = take(9), take(1)[0]
     gathered, xp, xq = take(3)
     hidden, grads, cots = take(3), take(4), take(2)
+    near, away = take(4), take(4)
     target, diff, scale, part_sums, marked = take(5)
     unit_refs = [take(5) for _ in range(6)]
     ring_refs = [take(5) for _ in range(2)]
@@ -297,7 +330,7 @@
     mine, turn = places.rows[0], ring.rows[0]
     units = [Unit(links, places, r) for r in unit_refs]
     rings = [Unit(links, ring, r) for r in ring_refs]
-    layers = ((2, 3), (0, 1), (1, 2))
+    layers = ((2, (1, 2, 3, 3)), (0, (1,)), (1, (6, 5)))
     pieces = {layer: cuts(units[2 * layer].width, n) for layer, n in layers}
     out = []
 
@@ -349,12 +382,15 @@
 
             def body(cols):
                 g, u = gate.value(cols), up.value(cols)
-                hidden[layer][mine, cols] = (g * jax.nn.sigmoid(g) * u).astype(
-                    jnp.bfloat16
-                )
+                sig = jax.nn.sigmoid(g)
+                slope = g * sig
+                hidden[layer][mine, cols] = (slope * u).astype(jnp.bfloat16)
                 if layer < 2:
-                    gate.own[gate.half :, cols] = g
-                    up.own[up.half :, cols] = u
+                    bend = u * sig * (1.0 + g * (1.0 - sig))
+                    gate.own[gate.half :, cols] = bend
+                    up.own[up.half :, cols] = slope
+                    near[2 * layer][:, cols] = bend.astype(jnp.bfloat16)
+                    near[2 * layer + 1][:, cols] = slope.astype(jnp.bfloat16)
 
             tiles(piece, body)
             spreads[layer, piece] = Spread(links, hidden[layer], places, piece)
@@ -381,7 +417,7 @@
 
             tiles(wide, body, 256)
 
-        halves = cuts(target.shape[1], 2)
+        halves = cuts(target.shape[1], (1, 1))
         for piece in pieces[2]:
             activate(2, piece)
         for piece in pieces[0]:
@@ -402,6 +438,7 @@
             rings[0].take(diff, half)
         for piece in pieces[1]:
             activate(1, piece)
+        lent = [links.copy(near[i], away[i], places.to(2)) for i in range(4)]
         for half in halves:
             rings[0].forward(half)
         for piece in pieces[1]:
@@ -427,38 +464,44 @@
             turns.append(Spread(links, cots[i], ring))
             sums.append(0.5 * total_sum)
 
-        back = []
+        back, parcels = [], [[], []]
         for i in range(2):
             gate, up = units[2 * i], units[2 * i + 1]
-            back.append(
-                Unit(links, places, (gate.snd1, up.snd1, gate.rcv1, gate.snd2, gate.rcv2))
-            )
+            pair = ((up.snd2, gate.snd2), (up.rcv2, gate.rcv2))
+            back.append(Exchange(links, places, (gate.snd1, up.snd1, gate.rcv1, *pair)))
             gate.settle()
             up.settle()
-        gates = {}
-
-        def differentiate(i):
-            whole = (0, back[i].width)
-            back[i].ready(whole)
-            gate, up = units[2 * i], units[2 * i + 1]
-            half = gate.half
+
+        def differentiate(i, piece):
+            back[i].ready(piece)
+            half = back[i].half
 
             def body(cols):
-                b = back[i].value(cols)
-                g, u = gate.own[half:, cols], up.own[half:, cols]
-                sig = jax.nn.sigmoid(g)
-                dgate = b * u * sig * (1.0 + g * (1.0 - sig))
-                grads[2 * i][mine, cols] = dgate.astype(jnp.bfloat16)
-                grads[2 * i + 1][mine, cols] = (b * g * sig).astype(jnp.bfloat16)
-
-            tiles(whole, body)
-            gates[i] = [Spread(links, grads[2 * i + j], places) for j in range(2)]
+                for k, rows in enumerate((places.rows[2], mine)):
+                    value = back[i].value(k, cols)
+                    for j in range(2):
+                        factor = units[2 * i + j].own[half:, cols] if k else away[2 * i + j][:, cols]
+                        out = value * factor.astype(jnp.float32)
+                        grads[2 * i + j][rows, cols] = out.astype(jnp.bfloat16)
+
+            tiles(piece, body)
+            for j in range(2):
+                for rows in (places.rows[2], mine):
+                    spot = part(grads[2 * i + j], piece, rows)
+                    parcels[i].append(links.copy(spot, spot, places.to(1)))
+
+        def collect(i):
+            for made in parcels[i]:
+                made.wait_recv()
+            for j in range(2):
+                out.append(stores.copy(grads[2 * i + j], kept_out[5 + 2 * i + j]))
 
         def back_project(i, left):
             turns[i].finish()
             out.append(stores.copy(cots[i], kept_out[3 + i]))
             arrange(left, cots[i], places)
-            back[i].multiply(left, dbuf[i], True, (0, back[i].width))
+            for piece in pieces[i]:
+                back[i].multiply(left, dbuf[i], True, piece)
 
         cotangent(0)
         for half in halves:
@@ -471,32 +514,29 @@
             links.copy((part_sums, 0), (part_sums, k), ring.to(k)) for k in (1, 2, 3)
         ]
         back_project(0, xp)
-        back[0].forward((0, back[0].width))
+        for piece in pieces[0]:
+            back[0].forward(piece)
         turns[1].relay()
-        differentiate(0)
         back_project(1, xq)
-        back[1].forward((0, back[1].width))
+        for piece in pieces[1]:
+            back[1].forward(piece)
+        for made in lent:
+            made.wait_recv()
+        for piece in pieces[0]:
+            differentiate(0, piece)
         for move in parts:
             move.wait_recv()
         marked[0] = part_sums[0] + part_sums[1] + part_sums[2] + part_sums[3]
         marks = [
             links.copy((marked, 0), (marked, k), places.to(k)) for k in (1, 2, 3)
         ]
-        for spread in gates[0]:
-            spread.relay()
-        differentiate(1)
+        collect(0)
+        for piece in pieces[1]:
+            differentiate(1, piece)
         for mark in marks:
             mark.wait_recv()
         loss[...] = marked[0] + marked[1] + marked[2] + marked[3]
-        for j, spread in enumerate(gates[0]):
-            spread.finish()
-            out.append(stores.copy(grads[j], kept_out[5 + j]))
-        for spread in gates[1]:
-            spread.relay()
-        for j, spread in enumerate(gates[1]):
-            spread.finish()
-            out.append(stores.copy(grads[2 + j], kept_out[7 + j]))
-
+        collect(1)
         for made in out:
             made.wait()
         links.drain()
@@ -518,6 +558,7 @@
     scratch += [pltpu.VMEM((rows, w), bf16) for w in widths]
     scratch += [pltpu.VMEM((rows, widths[i // 2]), bf16) for i in range(4)]
     scratch += [pltpu.VMEM((rows, depth), bf16)] * 2
+    scratch += [pltpu.VMEM((block, widths[i // 2]), bf16) for i in range(4)] * 2
     scratch += [pltpu.VMEM((rows, depth), f32)] * 2
     scratch += [pltpu.VMEM((rows, 128), f32)]
     scratch += [pltpu.VMEM((4, 8, 128), f32)] * 2

time: 135 us -> 125 us (0.926); the launches traced: 133 us -> 125 us
  Pallas kernels: 132 us -> 124 us
    pallas_call x1, Pallas kernels: 120 us -> 112 us  [layer_call(): pl.pallas_call(functools.partial(layer_kernel, flips), out_shape=outs, in...]
where the time goes in v3:
time: 125 us
  Pallas kernels  124 us (99%)
    pallas_call x1, Pallas kernels, layer_call(): pl.pallas_call(functools.partial(layer_kernel, flips), out_shape=outs, in...  112 us
    pallas_call x1, Pallas kernels, gradient_call(): pl.pallas_call(functools.partial(gradient_kernel, jobs), out_shape=outs +...  12 us

profile of v3, /device:TPU:1, one launch (start us, length us, event | category | flops | bytes accessed | tf_op | source)
XLA Modules:
  0.0 125.0 jit_solution(2640424167264186461)
XLA Ops:
  0.6 112.2 %shard_map.162 = (bf16[192,1280]{1,0:T(8,128)(2,1)}, bf16[192,1728]{1,0:T(8,128)(2,1)}, bf16[192,1408]{1,0:T(8,128)(2,1)}, bf16[192,1280]{1,0:T(8,128)(2,1)}, bf...) custom-call(bf16[48,1280]{1,0:T(8,128)(2,1)} %refs_0_.1, ...), custom_call_target="tpu_custom_call" | custom-call | tf_op jit(solution)/shard_map/pallas_call | solution.py:572
  112.9 12.0 %shard_map.163 = (bf16[1728,1280]{1,0:T(8,128)(2,1)}, bf16[1408,1280]{1,0:T(8,128)(2,1)}, bf16[1728,1280]{1,0:T(8,128)(2,1)}, bf16[1728,1280]{1,0:T(8,128)(2,1)}...) custom-call(bf16[192,1280]{1,0:T(8,128)(2,1)} %get-tuple-element.24.refs_0_, ...), custom_call_target="tpu_custom_call" | custom-call | tf_op jit(solution)/shard_map/pallas_call | solution.py:622

commit v4 on v3

--- a/solution.py
+++ b/solution.py
@@ -57,14 +57,14 @@
         self.args = args
 
     def build(self):
-        src, dst, send, recv, at, device = self.args
+        src, dst, send, recv, at, land, device = self.args
         if device is None:
-            return pltpu.make_async_copy(view(src), view(dst), recv.at[at])
+            return pltpu.make_async_copy(view(src), view(dst), recv.at[land])
         return pltpu.make_async_remote_copy(
             src_ref=view(src),
             dst_ref=view(dst),
             send_sem=send.at[at],
-            recv_sem=recv.at[at],
+            recv_sem=recv.at[land],
             device_id=device,
             device_id_type=MESH,
         )
@@ -84,11 +84,16 @@
         self.send, self.recv, self.count, self.made = send, recv, 0, []
 
     def copy(self, src, dst, device=None):
-        made = Move(src, dst, self.send, self.recv, self.count, device)
-        self.count += 1
+        at = self.reserve(1)
+        made = Move(src, dst, self.send, self.recv, at, at, device)
         made.build().start()
         self.made.append(made)
         return made
+
+    def reserve(self, count):
+        at = self.count
+        self.count += count
+        return at
 
     def settle(self, made):
         made.wait_send()
@@ -189,16 +194,6 @@
         tiles(piece, body)
         self.pass_on(piece)
 
-    def take(self, source, piece):
-        me, sib, far, diag = self.places.rows
-        half = self.half
-        cols = pl.ds(*piece)
-        for i, rows in enumerate((diag, sib)):
-            self.snd1[i * half : (i + 1) * half, cols] = source[rows, cols].astype(self.snd1.dtype)
-        for i, rows in enumerate((far, me)):
-            self.own[i * half : (i + 1) * half, cols] = source[rows, cols]
-        self.pass_on(piece)
-
     def forward(self, piece):
         self.first[piece].wait_recv()
         half = self.half
@@ -287,6 +282,140 @@
     def finish(self):
         self.side.wait_recv()
         self.last.wait_recv()
+
+
+class Line:
+    def __init__(self, links, ring):
+        self.links, self.ring = links, ring
+        self.end = ring.me // 2 == ring.me % 2
+        self.sent = {True: [], False: []}
+
+    def at_end(self, body):
+        pl.when(self.end)(body)
+
+    def at_middle(self, body):
+        pl.when(jnp.logical_not(self.end))(body)
+
+    def send(self, end, src, dst, k, land):
+        links = self.links
+        made = Move(src, dst, links.send, links.recv, links.reserve(1), land, self.ring.to(k))
+        made.build().start()
+        self.sent[end].append(made)
+
+    def arrive(self, dst, land):
+        links = self.links
+        Move(dst, dst, links.send, links.recv, land, land, self.ring.to(1)).wait_recv()
+
+    def drain(self):
+        @self.at_end
+        def _():
+            for made in self.sent[True]:
+                made.wait_send()
+
+        @self.at_middle
+        def _():
+            for made in self.sent[False]:
+                made.wait_send()
+
+
+class LineSum:
+    def __init__(self, line, source, halves, refs):
+        self.line, self.source, self.rows = line, source, line.ring.rows
+        self.snd, self.rcv, self.total = refs
+        self.lands = {half: line.links.reserve(5) for half in halves}
+
+    def push(self, end, half, k, place, held, to, slot):
+        cols = pl.ds(*half)
+        value = self.source[self.rows[place], cols]
+        if held is not None:
+            value = value + self.rcv[held, :, cols].astype(jnp.float32)
+        self.snd[k, :, cols] = value.astype(jnp.bfloat16)
+        dst = (self.rcv, (slot, slice(None), cols))
+        src = (self.snd, (k, slice(None), cols))
+        self.line.send(end, src, dst, to, self.lands[half] + slot)
+
+    def arrive(self, half, slot):
+        dst = (self.rcv, (slot, slice(None), pl.ds(*half)))
+        self.line.arrive(dst, self.lands[half] + slot)
+
+    def start(self, half):
+        @self.line.at_end
+        def _():
+            for k, place in enumerate((3, 2, 1)):
+                self.push(True, half, k, place, None, 1, k)
+
+    def hop(self, half, k):
+        @self.line.at_middle
+        def _():
+            self.arrive(half, k)
+            self.push(False, half, k, 2 + k, k, 3, 3 + k)
+
+    def turn(self, half):
+        @self.line.at_middle
+        def _():
+            self.arrive(half, 3)
+            self.push(False, half, 2, 1, 3, 1, 0)
+
+    def finish(self, half):
+        cols = pl.ds(*half)
+
+        def gather(slots):
+            value = self.source[self.rows[0], cols]
+            for slot in slots:
+                self.arrive(half, slot)
+                value = value + self.rcv[slot, :, cols].astype(jnp.float32)
+            self.total[:, cols] = value
+
+        self.line.at_end(lambda: gather((0,)))
+        self.line.at_middle(lambda: gather((2, 4)))
+        return self.total[:, cols]
+
+
+class LineSpread:
+    def __init__(self, line, ref, halves, source=None):
+        self.line, self.ref, self.source, self.rows = line, ref, source, line.ring.rows
+        self.lands = {half: line.links.reserve(3) - 1 for half in halves}
+
+    def spot(self, half, place):
+        return part(self.ref, half, self.rows[place])
+
+    def push(self, end, half, place, to, origin):
+        dst = self.spot(half, place)
+        src = dst if place or self.source is None else part(self.source, half)
+        self.line.send(end, src, dst, to, self.lands[half] + origin)
+
+    def arrive(self, half, place):
+        self.line.arrive(self.spot(half, place), self.lands[half] + place)
+
+    def start(self, half):
+        @self.line.at_end
+        def _():
+            self.push(True, half, 0, 1, 1)
+
+        @self.line.at_middle
+        def _():
+            self.push(False, half, 0, 3, 3)
+            self.push(False, half, 0, 1, 1)
+
+    def hop(self, half):
+        @self.line.at_middle
+        def _():
+            self.arrive(half, 1)
+            self.push(False, half, 1, 3, 2)
+            self.arrive(half, 3)
+            self.push(False, half, 3, 1, 2)
+
+    def last(self, half):
+        @self.line.at_middle
+        def _():
+            self.arrive(half, 2)
+            self.push(False, half, 2, 1, 3)
+
+    def finish(self, half):
+        @self.line.at_end
+        def _():
+            for place in (1, 2, 3):
+                self.arrive(half, place)
 
 
 def arrange(dst, src, places):
@@ -322,14 +451,18 @@
     near, away = take(4), take(4)
     target, diff, scale, part_sums, marked = take(5)
     unit_refs = [take(5) for _ in range(6)]
-    ring_refs = [take(5) for _ in range(2)]
+    ring_refs = [take(3) for _ in range(2)]
     send, recv, wsem, dsem, osem = take(5)
 
     links, loads, stores = Links(send, recv), Links(None, wsem), Links(None, osem)
     places, ring = Places("split", tok.shape[0]), Places("mp", tok.shape[0])
     mine, turn = places.rows[0], ring.rows[0]
     units = [Unit(links, places, r) for r in unit_refs]
-    rings = [Unit(links, ring, r) for r in ring_refs]
+    line = Line(links, ring)
+    halves = cuts(target.shape[1], (1, 1))
+    rings = [LineSum(line, r, halves, refs) for r, refs in zip((diff, target), ring_refs)]
+    turns = [LineSpread(line, cot, halves) for cot in cots]
+    moves = LineSpread(line, gathered, halves, tok)
     layers = ((2, (1, 2, 3, 3)), (0, (1,)), (1, (6, 5)))
     pieces = {layer: cuts(units[2 * layer].width, n) for layer, n in layers}
     out = []
@@ -347,10 +480,12 @@
                     waits[i, piece] = loads.copy(src, dst)
         row_scale(scale, lengths)
         greet([spot.to(k) for spot in (places, ring) for k in (1, 2, 3)])
-        moves = Spread(links, gathered, ring, source=tok)
+        for half in halves:
+            moves.start(half)
         gathered[turn, :] = tok[...]
-        moves.relay()
-        moves.finish()
+        for step in (moves.hop, moves.last, moves.finish):
+            for half in halves:
+                step(half)
         out.append(stores.copy(gathered, kept_out[0]))
         arrange(xp, gathered, places)
         behind = None
@@ -417,7 +552,6 @@
 
             tiles(wide, body, 256)
 
-        halves = cuts(target.shape[1], (1, 1))
         for piece in pieces[2]:
             activate(2, piece)
         for piece in pieces[0]:
@@ -435,33 +569,36 @@
             project_down(0, piece, None if n else target, diff, False)
         out.append(stores.copy(hidden[0], kept_out[1]))
         for half in halves:
-            rings[0].take(diff, half)
+            rings[0].start(half)
         for piece in pieces[1]:
             activate(1, piece)
         lent = [links.copy(near[i], away[i], places.to(2)) for i in range(4)]
         for half in halves:
-            rings[0].forward(half)
-        for piece in pieces[1]:
+            rings[0].hop(half, 0)
+        for n, piece in enumerate(pieces[1]):
             spreads[1, piece].relay()
+            if n == 0:
+                for half in halves:
+                    rings[0].hop(half, 1)
+        for half in halves:
+            rings[0].turn(half)
         for n, piece in enumerate(pieces[1]):
             project_down(1, piece, None if n else target, target, False)
         out.append(stores.copy(hidden[1], kept_out[2]))
         for half in halves:
-            rings[1].take(target, half)
+            rings[1].start(half)
 
         factor = scale[turn, 0:1]
-        turns, sums = [], []
+        sums = []
 
         def cotangent(i):
             total_sum = 0.0
             for half in halves:
-                rings[i].ready(half)
-                cols = pl.ds(*half)
-                total = rings[i].value(cols)
+                total = rings[i].finish(half)
                 scaled = factor * total
-                cots[i][turn, cols] = scaled.astype(jnp.bfloat16)
+                cots[i][turn, pl.ds(*half)] = scaled.astype(jnp.bfloat16)
+                turns[i].start(half)
                 total_sum = total_sum + jnp.sum(scaled * total, keepdims=True)
-            turns.append(Spread(links, cots[i], ring))
             sums.append(0.5 * total_sum)
 
         back, parcels = [], [[], []]
@@ -497,7 +634,8 @@
                 out.append(stores.copy(grads[2 * i + j], kept_out[5 + 2 * i + j]))
 
         def back_project(i, left):
-            turns[i].finish()
+            for half in halves:
+                turns[i].finish(half)
             out.append(stores.copy(cots[i], kept_out[3 + i]))
             arrange(left, cots[i], places)
             for piece in pieces[i]:
@@ -505,8 +643,15 @@
 
         cotangent(0)
         for half in halves:
-            rings[1].forward(half)
-        turns[0].relay()
+            rings[1].hop(half, 0)
+        for half in halves:
+            turns[0].hop(half)
+        for half in halves:
+            rings[1].hop(half, 1)
+        for half in halves:
+            rings[1].turn(half)
+        for half in halves:
+            turns[0].last(half)
         cotangent(1)
         row = lax.broadcasted_iota(jnp.int32, part_sums.shape[1:], 0)
         part_sums[0] = jnp.where(row == 0, sums[0], sums[1])
@@ -514,9 +659,12 @@
             links.copy((part_sums, 0), (part_sums, k), ring.to(k)) for k in (1, 2, 3)
         ]
         back_project(0, xp)
+        for half in halves:
+            turns[1].hop(half)
         for piece in pieces[0]:
             back[0].forward(piece)
-        turns[1].relay()
+        for half in halves:
+            turns[1].last(half)
         back_project(1, xq)
         for piece in pieces[1]:
             back[1].forward(piece)
@@ -540,6 +688,7 @@
         for made in out:
             made.wait()
         links.drain()
+        line.drain()
 
     pl.run_scoped(rest, *[pltpu.VMEM(d.shape, jnp.bfloat16) for d in downs])
 
@@ -565,8 +714,9 @@
     for i in range(6):
         scratch += unit_scratch(rows, widths[i // 2])
     for _ in range(2):
-        scratch += unit_scratch(rows, depth, bf16)
-    copies = 120
+        scratch += [pltpu.VMEM((n, block, depth), bf16) for n in (3, 5)]
+        scratch += [pltpu.VMEM((block, depth), f32)]
+    copies = 220
     scratch += [pltpu.SemaphoreType.DMA((copies,))] * 2
     scratch += [pltpu.SemaphoreType.DMA((16,))] * 3
     return pl.pallas_call(

time: 125 us -> 127 us (1.016)
  no operation moved by 1% of the time
where the time goes in v4:
time: 127 us; the launch traced here: 126 us
  Pallas kernels  125 us (98%)
    pallas_call x1, Pallas kernels, layer_call(): pl.pallas_call(functools.partial(layer_kernel, flips), out_shape=outs, in...  113 us
    pallas_call x1, Pallas kernels, gradient_call(): pl.pallas_call(functools.partial(gradient_kernel, jobs), out_shape=outs +...  12 us

profile of v4, /device:TPU:1, one launch (start us, length us, event | category | flops | bytes accessed | tf_op | source)
XLA Modules:
  0.0 126.1 jit_solution(9551786612561740512)
XLA Ops:
  0.6 113.4 %shard_map.162 = (bf16[192,1280]{1,0:T(8,128)(2,1)}, bf16[192,1728]{1,0:T(8,128)(2,1)}, bf16[192,1408]{1,0:T(8,128)(2,1)}, bf16[192,1280]{1,0:T(8,128)(2,1)}, bf...) custom-call(bf16[48,1280]{1,0:T(8,128)(2,1)} %refs_0_.1, ...), custom_call_target="tpu_custom_call" | custom-call | tf_op jit(solution)/shard_map/pallas_call | solution.py:722
  114.0 12.0 %shard_map.163 = (bf16[1728,1280]{1,0:T(8,128)(2,1)}, bf16[1408,1280]{1,0:T(8,128)(2,1)}, bf16[1728,1280]{1,0:T(8,128)(2,1)}, bf16[1728,1280]{1,0:T(8,128)(2,1)}...) custom-call(bf16[192,1280]{1,0:T(8,128)(2,1)} %get-tuple-element.24.refs_0_, ...), custom_call_target="tpu_custom_call" | custom-call | tf_op jit(solution)/shard_map/pallas_call | solution.py:772

commit v5 on v4

--- a/solution.py
+++ b/solution.py
@@ -271,7 +271,7 @@
         piece = (0, ref.shape[1]) if piece is None else piece
         mine = part(ref, piece, places.rows[0])
         self.theirs = part(ref, piece, places.rows[2])
-        source = mine if source is None else source
+        source = mine if source is None else part(source, piece)
         self.out = links.copy(source, mine, places.to(2))
         self.side = links.copy(source, mine, places.to(1))
 
@@ -369,6 +369,32 @@
         self.line.at_end(lambda: gather((0,)))
         self.line.at_middle(lambda: gather((2, 4)))
         return self.total[:, cols]
+
+
+class DirectSum:
+    def __init__(self, line, source, refs):
+        self.links, self.ring, self.source = line.links, line.ring, source
+        self.snd, self.rcv = refs[:2]
+        self.made = {}
+
+    def start(self, half):
+        cols = pl.ds(*half)
+        moves = []
+        for place in (3, 2, 1):
+            spot = (place - 1, slice(None), cols)
+            self.snd[spot] = self.source[self.ring.rows[place], cols].astype(jnp.bfloat16)
+            moves.append(
+                self.links.copy((self.snd, spot), (self.rcv, spot), self.ring.to(place))
+            )
+        self.made[half] = moves
+
+    def finish(self, half):
+        cols = pl.ds(*half)
+        value = self.source[self.ring.rows[0], cols]
+        for slot, made in zip((2, 1, 0), self.made[half]):
+            made.wait_recv()
+            value = value + self.rcv[slot, :, cols].astype(jnp.float32)
+        return value
 
 
 class LineSpread:
@@ -459,10 +485,9 @@
     mine, turn = places.rows[0], ring.rows[0]
     units = [Unit(links, places, r) for r in unit_refs]
     line = Line(links, ring)
-    halves = cuts(target.shape[1], (1, 1))
-    rings = [LineSum(line, r, halves, refs) for r, refs in zip((diff, target), ring_refs)]
-    turns = [LineSpread(line, cot, halves) for cot in cots]
-    moves = LineSpread(line, gathered, halves, tok)
+    halves, slabs = cuts(target.shape[1], (1, 1)), cuts(target.shape[1], (6, 4))
+    rings = [LineSum(line, diff, halves, ring_refs[0]), DirectSum(line, target, ring_refs[1])]
+    turns = LineSpread(line, cots[0], halves)
     layers = ((2, (1, 2, 3, 3)), (0, (1,)), (1, (6, 5)))
     pieces = {layer: cuts(units[2 * layer].width, n) for layer, n in layers}
     out = []
@@ -480,12 +505,12 @@
                     waits[i, piece] = loads.copy(src, dst)
         row_scale(scale, lengths)
         greet([spot.to(k) for spot in (places, ring) for k in (1, 2, 3)])
-        for half in halves:
-            moves.start(half)
+        moves = [Spread(links, gathered, ring, half, tok) for half in halves]
         gathered[turn, :] = tok[...]
-        for step in (moves.hop, moves.last, moves.finish):
-            for half in halves:
-                step(half)
+        for move in moves:
+            move.relay()
+        for move in moves:
+            move.finish()
         out.append(stores.copy(gathered, kept_out[0]))
         arrange(xp, gathered, places)
         behind = None
@@ -585,21 +610,16 @@
         for n, piece in enumerate(pieces[1]):
             project_down(1, piece, None if n else target, target, False)
         out.append(stores.copy(hidden[1], kept_out[2]))
-        for half in halves:
-            rings[1].start(half)
+        for slab in slabs:
+            rings[1].start(slab)
 
         factor = scale[turn, 0:1]
-        sums = []
-
-        def cotangent(i):
-            total_sum = 0.0
-            for half in halves:
-                total = rings[i].finish(half)
-                scaled = factor * total
-                cots[i][turn, pl.ds(*half)] = scaled.astype(jnp.bfloat16)
-                turns[i].start(half)
-                total_sum = total_sum + jnp.sum(scaled * total, keepdims=True)
-            sums.append(0.5 * total_sum)
+
+        def cotangent(i, half):
+            total = rings[i].finish(half)
+            scaled = factor * total
+            cots[i][turn, pl.ds(*half)] = scaled.astype(jnp.bfloat16)
+            return 0.5 * jnp.sum(scaled * total, keepdims=True)
 
         back, parcels = [], [[], []]
         for i in range(2):
@@ -634,37 +654,38 @@
                 out.append(stores.copy(grads[2 * i + j], kept_out[5 + 2 * i + j]))
 
         def back_project(i, left):
-            for half in halves:
-                turns[i].finish(half)
             out.append(stores.copy(cots[i], kept_out[3 + i]))
             arrange(left, cots[i], places)
             for piece in pieces[i]:
                 back[i].multiply(left, dbuf[i], True, piece)
 
-        cotangent(0)
+        sums, relays = [0.0, 0.0], []
         for half in halves:
-            rings[1].hop(half, 0)
+            sums[0] = sums[0] + cotangent(0, half)
+            turns.start(half)
         for half in halves:
-            turns[0].hop(half)
-        for half in halves:
-            rings[1].hop(half, 1)
-        for half in halves:
-            rings[1].turn(half)
-        for half in halves:
-            turns[0].last(half)
-        cotangent(1)
+            turns.hop(half)
+        for n, slab in enumerate(slabs):
+            sums[1] = sums[1] + cotangent(1, slab)
+            relays.append(Spread(links, cots[1], ring, slab))
+            if n == 0:
+                for half in halves:
+                    turns.last(half)
         row = lax.broadcasted_iota(jnp.int32, part_sums.shape[1:], 0)
         part_sums[0] = jnp.where(row == 0, sums[0], sums[1])
         parts = [
             links.copy((part_sums, 0), (part_sums, k), ring.to(k)) for k in (1, 2, 3)
         ]
+        relays[0].relay()
+        for half in halves:
+            turns.finish(half)
         back_project(0, xp)
-        for half in halves:
-            turns[1].hop(half)
+        for relay in relays[1:]:
+            relay.relay()
         for piece in pieces[0]:
             back[0].forward(piece)
-        for half in halves:
-            turns[1].last(half)
+        for relay in relays:
+            relay.finish()
         back_project(1, xq)
         for piece in pieces[1]:
             back[1].forward(piece)

time: 127 us -> 136 us (1.071)
  Pallas kernels: 125 us -> 134 us
    pallas_call x1, Pallas kernels: 113 us -> 122 us  [layer_call(): pl.pallas_call(functools.partial(layer_kernel, flips), out_shape=outs, in...]
where the time goes in v5:
time: 136 us; the launch traced here: 134 us
  Pallas kernels  134 us (99%)
    pallas_call x1, Pallas kernels, layer_call(): pl.pallas_call(functools.partial(layer_kernel, flips), out_shape=outs, in...  122 us
    pallas_call x1, Pallas kernels, gradient_call(): pl.pallas_call(functools.partial(gradient_kernel, jobs), out_shape=outs +...  12 us

profile of v5, /device:TPU:1, one launch (start us, length us, event | category | flops | bytes accessed | tf_op | source)
XLA Modules:
  0.0 134.4 jit_solution(15588055209339275696)
XLA Ops:
  0.6 121.6 %shard_map.162 = (bf16[192,1280]{1,0:T(8,128)(2,1)}, bf16[192,1728]{1,0:T(8,128)(2,1)}, bf16[192,1408]{1,0:T(8,128)(2,1)}, bf16[192,1280]{1,0:T(8,128)(2,1)}, bf...) custom-call(bf16[48,1280]{1,0:T(8,128)(2,1)} %refs_0_.1, ...), custom_call_target="tpu_custom_call" | custom-call | tf_op jit(solution)/shard_map/pallas_call | solution.py:743
  122.3 12.0 %shard_map.163 = (bf16[1728,1280]{1,0:T(8,128)(2,1)}, bf16[1408,1280]{1,0:T(8,128)(2,1)}, bf16[1728,1280]{1,0:T(8,128)(2,1)}, bf16[1728,1280]{1,0:T(8,128)(2,1)}...) custom-call(bf16[192,1280]{1,0:T(8,128)(2,1)} %get-tuple-element.24.refs_0_, ...), custom_call_target="tpu_custom_call" | custom-call | tf_op jit(solution)/shard_map/pallas_call | solution.py:793

commit v6 on v3

--- a/solution.py
+++ b/solution.py
@@ -10,7 +10,7 @@
 MESH = pl.DeviceIdType.MESH
 VMEM = pl.BlockSpec(memory_space=pltpu.VMEM)
 ANY = pl.BlockSpec(memory_space=pl.ANY)
-TILE = 384
+TILE = 768
 GRANT = 67043328
 
 LEN = 64
@@ -330,7 +330,7 @@
     mine, turn = places.rows[0], ring.rows[0]
     units = [Unit(links, places, r) for r in unit_refs]
     rings = [Unit(links, ring, r) for r in ring_refs]
-    layers = ((2, (1, 2, 3, 3)), (0, (1,)), (1, (6, 5)))
+    layers = ((2, (3, 6, 9, 9)), (0, (1,)), (1, (6, 5)))
     pieces = {layer: cuts(units[2 * layer].width, n) for layer, n in layers}
     out = []
 
@@ -415,7 +415,7 @@
                 else:
                     dst[:, cols] = out - first[:, cols]
 
-            tiles(wide, body, 256)
+            tiles(wide, body, 1280)
 
         halves = cuts(target.shape[1], (1, 1))
         for piece in pieces[2]:
@@ -439,10 +439,12 @@
         for piece in pieces[1]:
             activate(1, piece)
         lent = [links.copy(near[i], away[i], places.to(2)) for i in range(4)]
-        for half in halves:
+        for n, piece in enumerate(pieces[1]):
+            spreads[1, piece].relay()
+            if n < len(halves):
+                rings[0].forward(halves[n])
+        for half in halves[len(pieces[1]) :]:
             rings[0].forward(half)
-        for piece in pieces[1]:
-            spreads[1, piece].relay()
         for n, piece in enumerate(pieces[1]):
             project_down(1, piece, None if n else target, target, False)
         out.append(stores.copy(hidden[1], kept_out[2]))
@@ -450,19 +452,16 @@
             rings[1].take(target, half)
 
         factor = scale[turn, 0:1]
-        turns, sums = [], []
-
-        def cotangent(i):
-            total_sum = 0.0
-            for half in halves:
-                rings[i].ready(half)
-                cols = pl.ds(*half)
-                total = rings[i].value(cols)
-                scaled = factor * total
-                cots[i][turn, cols] = scaled.astype(jnp.bfloat16)
-                total_sum = total_sum + jnp.sum(scaled * total, keepdims=True)
-            turns.append(Spread(links, cots[i], ring))
-            sums.append(0.5 * total_sum)
+        turns, sums = ([], []), [0.0, 0.0]
+
+        def cotangent(i, half):
+            rings[i].ready(half)
+            cols = pl.ds(*half)
+            total = rings[i].value(cols)
+            scaled = factor * total
+            cots[i][turn, cols] = scaled.astype(jnp.bfloat16)
+            turns[i].append(Spread(links, cots[i], ring, half))
+            sums[i] = sums[i] + 0.5 * jnp.sum(scaled * total, keepdims=True)
 
         back, parcels = [], [[], []]
         for i in range(2):
@@ -497,26 +496,31 @@
                 out.append(stores.copy(grads[2 * i + j], kept_out[5 + 2 * i + j]))
 
         def back_project(i, left):
-            turns[i].finish()
+            for made in turns[i]:
+                made.finish()
             out.append(stores.copy(cots[i], kept_out[3 + i]))
             arrange(left, cots[i], places)
             for piece in pieces[i]:
                 back[i].multiply(left, dbuf[i], True, piece)
 
-        cotangent(0)
         for half in halves:
+            cotangent(0, half)
             rings[1].forward(half)
-        turns[0].relay()
-        cotangent(1)
+        for made in turns[0]:
+            made.relay()
+        cotangent(1, halves[0])
+        back_project(0, xp)
+        for half in halves[1:]:
+            cotangent(1, half)
+        for piece in pieces[0]:
+            back[0].forward(piece)
+        for made in turns[1]:
+            made.relay()
         row = lax.broadcasted_iota(jnp.int32, part_sums.shape[1:], 0)
         part_sums[0] = jnp.where(row == 0, sums[0], sums[1])
         parts = [
             links.copy((part_sums, 0), (part_sums, k), ring.to(k)) for k in (1, 2, 3)
         ]
-        back_project(0, xp)
-        for piece in pieces[0]:
-            back[0].forward(piece)
-        turns[1].relay()
         back_project(1, xq)
         for piece in pieces[1]:
             back[1].forward(piece)
@@ -566,9 +570,9 @@
         scratch += unit_scratch(rows, widths[i // 2])
     for _ in range(2):
         scratch += unit_scratch(rows, depth, bf16)
-    copies = 120
+    copies = 160
     scratch += [pltpu.SemaphoreType.DMA((copies,))] * 2
-    scratch += [pltpu.SemaphoreType.DMA((16,))] * 3
+    scratch += [pltpu.SemaphoreType.DMA((24,))] * 3
     return pl.pallas_call(
         functools.partial(layer_kernel, flips),
         out_shape=outs,

time: 125 us -> 123 us (0.984)
  Pallas kernels: 124 us -> 122 us
    pallas_call x1, Pallas kernels: 112 us -> 110 us  [layer_call(): pl.pallas_call(functools.partial(layer_kernel, flips), out_shape=outs, in...]
where the time goes in v6:
time: 123 us
  Pallas kernels  122 us (99%)
    pallas_call x1, Pallas kernels, layer_call(): pl.pallas_call(functools.partial(layer_kernel, flips), out_shape=outs, in...  110 us
    pallas_call x1, Pallas kernels, gradient_call(): pl.pallas_call(functools.partial(gradient_kernel, jobs), out_shape=outs +...  12 us

profile of v6, /device:TPU:1, one launch (start us, length us, event | category | flops | bytes accessed | tf_op | source)
XLA Modules:
  0.0 122.8 jit_solution(8924855884632391740)
XLA Ops:
  0.6 110.0 %shard_map.162 = (bf16[192,1280]{1,0:T(8,128)(2,1)}, bf16[192,1728]{1,0:T(8,128)(2,1)}, bf16[192,1408]{1,0:T(8,128)(2,1)}, bf16[192,1280]{1,0:T(8,128)(2,1)}, bf...) custom-call(bf16[48,1280]{1,0:T(8,128)(2,1)} %refs_0_.1, ...), custom_call_target="tpu_custom_call" | custom-call | tf_op jit(solution)/shard_map/pallas_call | solution.py:576
  110.7 12.0 %shard_map.163 = (bf16[1728,1280]{1,0:T(8,128)(2,1)}, bf16[1408,1280]{1,0:T(8,128)(2,1)}, bf16[1728,1280]{1,0:T(8,128)(2,1)}, bf16[1728,1280]{1,0:T(8,128)(2,1)}...) custom-call(bf16[192,1280]{1,0:T(8,128)(2,1)} %get-tuple-element.24.refs_0_, ...), custom_call_target="tpu_custom_call" | custom-call | tf_op jit(solution)/shard_map/pallas_call | solution.py:626

commit v7 on v6

--- a/solution.py
+++ b/solution.py
@@ -10,7 +10,7 @@
 MESH = pl.DeviceIdType.MESH
 VMEM = pl.BlockSpec(memory_space=pltpu.VMEM)
 ANY = pl.BlockSpec(memory_space=pl.ANY)
-TILE = 768
+TILE = 1152
 GRANT = 67043328
 
 LEN = 64
@@ -330,7 +330,7 @@
     mine, turn = places.rows[0], ring.rows[0]
     units = [Unit(links, places, r) for r in unit_refs]
     rings = [Unit(links, ring, r) for r in ring_refs]
-    layers = ((2, (3, 6, 9, 9)), (0, (1,)), (1, (6, 5)))
+    layers = ((2, (3, 6, 9, 9)), (0, (1,)), (1, (7, 4)))
     pieces = {layer: cuts(units[2 * layer].width, n) for layer, n in layers}
     out = []
 

time: 123 us -> 122 us (level)
  no operation moved by 1% of the time
where the time goes in v7:
time: 122 us
  Pallas kernels  121 us (99%)
    pallas_call x1, Pallas kernels, layer_call(): pl.pallas_call(functools.partial(layer_kernel, flips), out_shape=outs, in...  109 us
    pallas_call x1, Pallas kernels, gradient_call(): pl.pallas_call(functools.partial(gradient_kernel, jobs), out_shape=outs +...  12 us

profile of v7, /device:TPU:1, one launch (start us, length us, event | category | flops | bytes accessed | tf_op | source)
XLA Modules:
  0.0 121.6 jit_solution(8110518266872805734)
XLA Ops:
  0.6 108.8 %shard_map.162 = (bf16[192,1280]{1,0:T(8,128)(2,1)}, bf16[192,1728]{1,0:T(8,128)(2,1)}, bf16[192,1408]{1,0:T(8,128)(2,1)}, bf16[192,1280]{1,0:T(8,128)(2,1)}, bf...) custom-call(bf16[48,1280]{1,0:T(8,128)(2,1)} %refs_0_.1, ...), custom_call_target="tpu_custom_call" | custom-call | tf_op jit(solution)/shard_map/pallas_call | solution.py:576
  109.4 12.0 %shard_map.163 = (bf16[1728,1280]{1,0:T(8,128)(2,1)}, bf16[1408,1280]{1,0:T(8,128)(2,1)}, bf16[1728,1280]{1,0:T(8,128)(2,1)}, bf16[1728,1280]{1,0:T(8,128)(2,1)}...) custom-call(bf16[192,1280]{1,0:T(8,128)(2,1)} %get-tuple-element.24.refs_0_, ...), custom_call_target="tpu_custom_call" | custom-call | tf_op jit(solution)/shard_map/pallas_call | solution.py:626
